TPU v7x, 128 devices: a whole 4x4x4 slice. The times are simulated.
128 devices in a mesh: row: 16 (over z, x), col: 8 (over y, core).
Axes of the slice: x: 4, y: 4, z: 4, core: 2. Of those that a mesh axis runs over, the one named last changes fastest.
Arguments:
- density: bfloat16 [192, 24, 128, 128], P('row'), may hold values from -4 to 4
- slot_cols: int32 [192, 24], replicated, may hold values from -1 to 191, as said below
Outputs:
- purified: bfloat16 [192, 24, 128, 128], P('row', 'col')
Inputs may be any that keep to these rules, and one draw needn't show every extreme that they name: `slot_cols`: slots c * 3 to c * 3 + 2 of a block row name distinct block columns of c * 24 to c * 24 + 23, or -1. Within one such range of slots, block rows t * 12 to t * 12 + 11 have at most 28 occupied slots together, exactly 28 for some t and c.
All inputs are finite; a program needn't handle non-finite values.
Results may differ from a plain program's by a relative error of at most 0.0047.
Values may be sent and summed in bfloat16 or wider, within the bound.
A program may use at most 192 MiB of HBM per device.

v0:
```python
import jax
import jax.numpy as jnp
from jax import lax
from jax.sharding import PartitionSpec as P


def pick_rows(wanted, panel_flat, group_cols):
    block_rows, group_slots = group_cols.shape
    targets = jnp.arange(block_rows, dtype=jnp.int32)
    onehot = wanted[:, None] == targets[None, :]
    picked = jnp.dot(
        onehot.astype(jnp.bfloat16), panel_flat, preferred_element_type=jnp.float32
    ).astype(jnp.bfloat16)
    picked_cols = jnp.sum(jnp.where(onehot[:, :, None], group_cols[None, :, :], 0), axis=1)
    picked_cols = jnp.where(wanted[:, None] >= 0, picked_cols, -1)
    return (picked, picked_cols)


def selector(picked_cols, own_cols):
    match = picked_cols[..., :, None] == own_cols[..., None, :]
    match = match & (own_cols >= 0)[..., None, :] & (picked_cols >= 0)[..., :, None]
    return match.astype(jnp.float32)


def contract(left_band, panel, band_cols, own_cols, group_cols):
    band_rows, slot_count = band_cols.shape
    block_rows, group_slots = group_cols.shape
    block_size = panel.shape[-1]
    panel_flat = panel.reshape(block_rows, group_slots * block_size * block_size)
    group_size = 4
    group_count = band_rows // group_size

    def one_group(inputs):
        left_group, cols_group, own_group = inputs
        picked, picked_cols = pick_rows(
            cols_group.reshape(group_size * slot_count), panel_flat, group_cols
        )
        picked = picked.reshape(group_size, slot_count, group_slots, block_size, block_size)
        picked_cols = picked_cols.reshape(group_size, slot_count, group_slots)
        weights = selector(picked_cols, own_group[:, None, :])
        products = jnp.einsum(
            "itab,itubc->ituac", left_group, picked, preferred_element_type=jnp.float32
        )
        return jnp.einsum("itus,ituac->isac", weights, products, precision=lax.Precision.HIGHEST)

    result = lax.map(
        one_group,
        (
            left_band.reshape(group_count, group_size, slot_count, block_size, block_size),
            band_cols.reshape(group_count, group_size, slot_count),
            own_cols.reshape(group_count, group_size, group_slots),
        ),
    )
    return result.reshape(band_rows, group_slots, block_size, block_size)


def local(density, slot_cols):
    band_rows, slot_count, block_size = (density.shape[0], density.shape[1], density.shape[2])
    col_count = lax.axis_size("col")
    row_here = lax.axis_index("row")
    col_here = lax.axis_index("col")
    group_slots = slot_count // col_count
    block_rows = slot_cols.shape[0]
    tile_cells = band_rows * group_slots
    band_cols = lax.dynamic_slice_in_dim(slot_cols, row_here * band_rows, band_rows, 0)
    band_live = band_cols >= 0
    masked_band = density * band_live[:, :, None, None].astype(jnp.bfloat16)
    own_cols = lax.dynamic_slice_in_dim(band_cols, col_here * group_slots, group_slots, 1)
    own_tile = lax.dynamic_slice_in_dim(masked_band, col_here * group_slots, group_slots, 1)
    group_cols = lax.dynamic_slice_in_dim(slot_cols, col_here * group_slots, group_slots, 1)
    column_panel = lax.all_gather(
        own_tile.reshape(tile_cells, block_size, block_size), "row", axis=0, tiled=True
    )
    panel = column_panel.reshape(block_rows, group_slots, block_size, block_size)
    square = contract(masked_band, panel, band_cols, own_cols, group_cols)
    square_half = square.astype(jnp.bfloat16)
    square_band = lax.all_gather(square_half, "col", axis=1, tiled=True)
    cube_term = contract(square_band, panel, band_cols, own_cols, group_cols)
    return (3.0 * square - 2.0 * cube_term).astype(jnp.bfloat16)


def solution(mesh):
    return jax.shard_map(
        local,
        mesh=mesh,
        in_specs=(P("row", None, None, None), P()),
        out_specs=P("row", "col", None, None),
        check_vma=False,
    )
```

profile of v0, /device:TPU:0, one launch (start us, length us, event | category | flops | bytes accessed | tf_op | source)
XLA Modules:
  0.0 619.5 jit_solution(9663330189767109383)
XLA Ops:
  6.5 0.8 constant_dynamic-slice_fusion.4
  7.3 0.1 copy.74
  7.4 7.9 %broadcast_multiply_fusion = bf16[12,24,128,128]{3,2,1,0:T(8,128)(2,1)} fusion(bf16[12,24,128,128]{3,2,1,0:T(8,128)(2,1)} %param.6, bf16[12,24]{1,0:T(8,128)(2,1)S(1)} %compare_convert_fusion), kind=kLoop, calls=%fused_computation.48 | loop fusion | flops 4718592 | bytes 18874944 | tf_op jit(solution)/shard_map/mul | solution.py:67
  15.4 2.4 constant_dynamic-slice_fusion.2
  17.9 0.8 dynamic_slice.35
  18.7 0.1 reshape.179
  18.8 0.1 copy.62
  18.9 0.7 constant_dynamic-slice_fusion.3
  19.6 122.9 %all-gather.3.cloned.1.call-done = bf16[576,128,128]{2,1,0:T(8,128)(2,1)} async-done(((bf16[36,128,128]{2,1,0:T(8,128)(2,1)}), bf16[576,128,128]{2,1,0:T(8,128)(2,1)}) %all-gather.3.cloned.1.call-update) | async-done | bytes 18874384 | tf_op jit(solution)/shard_map/all_gather | solution.py:71
  142.5 24.5 %reshape_reshape.4 = bf16[192,49152]{1,0:T(8,128)(2,1)} reshape(bf16[576,128,128]{2,1,0:T(8,128)(2,1)} %all-gather.3.cloned.1.call-done) | data formatting | bytes 37748736 | tf_op jit(solution)/shard_map/reshape;reshape | solution.py:29
  167.0 0.5 broadcast.126.clone
  167.5 189.3 %while.20 = (s32[]{:T(128)}, f32[3,4,3,128,128]{4,2,3,1,0:T(4,128)S(1)}, s32[3,4,24]{2,1,0:T(4,128)S(1)}, s32[192,3]{0,1:T(4,128)S(1)}, s32[3,4,3]{2,1,0:T(4,128...) while((s32[]{:T(128)}, f32[3,4,3,128,128]{4,2,3,1,0:T(4,128)S(1)}, ...), condition=%wide.region_2.3_spmd, body=%wide.region_0.2_spmd.sunk | while | flops 3194637056 | bytes 136378496 | solution.py:46
  167.6 0.1 eq.133
  167.7 12.5 %fusion.51 = bf16[12,8,384,128]{3,1,2,0:T(8,128)(2,1)} fusion(bf16[192,49152]{1,0:T(8,128)(2,1)} %get-tuple-element.322, s32[96]{0:T(128)S(1)} %eq.133), kind=kOutput, calls=%fused_computation.2.clone.1 | convolution fusion | flops 1816676352 | bytes 28311936 | tf_op jit(solution)/shard_map/while/body/eval_jaxpr/dot_general | solution.py:11
  180.2 10.0 %copy.85 = bf16[12,8,384,128]{3,2,1,0:T(8,128)(2,1)} copy(bf16[12,8,384,128]{3,1,2,0:T(8,128)(2,1)} %fusion.51) | data formatting | bytes 18874368 | tf_op jit(solution)/shard_map/while
  190.2 10.8 %convolution_bitcast_fusion.6 = f32[4,24,3,128,128]{3,4,2,1,0:T(8,128)} fusion(bf16[4,24,3,128,128]{4,3,2,1,0:T(8,128)(2,1)} %bitcast.113, bf16[3,4,24,128,128]{4,3,2,1,0:T(8,128)(2,1)} %get-tuple-element.323, s32[]{:T(128)S(6)} %copy.97), kind=kOutput, calls=%fused_computation.1.clone.1 | convolution fusion | flops 1207959552 | bytes 31457284 | tf_op jit(solution)/shard_map/while/body/eval_jaxpr/itab,itubc->ituac/dot_general | solution.py:41
  201.0 18.8 %copy.86 = f32[4,24,3,128,128]{4,1,2,3,0:T(8,128)} copy(f32[4,24,3,128,128]{3,4,2,1,0:T(8,128)} %convolution_bitcast_fusion.6) | data formatting | bytes 37748736 | tf_op jit(solution)/shard_map/while/body/eval_jaxpr/itab,itubc->ituac/transpose | solution.py:41
  219.8 0.1 select_reduce_fusion.4
  220.0 0.1 reduce_sum.29
  220.1 10.5 %fusion.52 = f32[3,4,3,128,128]{4,2,3,1,0:T(4,128)S(1)} fusion(f32[3,4,3,128,128]{4,2,3,1,0:T(4,128)S(1)} %get-tuple-element.310, s32[]{:T(128)S(6)} %copy.97, f32[4,24,3,128,128]{4,1,2,3,0:T(8,128)} %copy.86, s32[4,3]{1,0:T(4,128)S(1)} %get-tuple-element.283, s32[4,24,3]{1,2,0:T(4,128)S(1)} %copy.87, pred[4,24,3]{1,2,0:T(4,128)(4,1)S(1)} %copy.88, ...), kind=kOutput, calls=%fused_computation.6.clone.1 | convolution fusion | flops 169871904 | bytes 19935748 | tf_op jit(solution)/shard_map/while/body/eval_jaxpr/itus,ituac->isac/dot_general | solution.py:44
  230.7 0.1 eq.133
  230.7 12.6 %fusion.51 = bf16[12,8,384,128]{3,1,2,0:T(8,128)(2,1)} fusion(bf16[192,49152]{1,0:T(8,128)(2,1)} %get-tuple-element.322, s32[96]{0:T(128)S(1)} %eq.133), kind=kOutput, calls=%fused_computation.2.clone.1 | convolution fusion | flops 1816676352 | bytes 28311936 | tf_op jit(solution)/shard_map/while/body/eval_jaxpr/dot_general | solution.py:11
  243.3 10.0 %copy.85 = bf16[12,8,384,128]{3,2,1,0:T(8,128)(2,1)} copy(bf16[12,8,384,128]{3,1,2,0:T(8,128)(2,1)} %fusion.51) | data formatting | bytes 18874368 | tf_op jit(solution)/shard_map/while
  253.3 10.8 %convolution_bitcast_fusion.6 = f32[4,24,3,128,128]{3,4,2,1,0:T(8,128)} fusion(bf16[4,24,3,128,128]{4,3,2,1,0:T(8,128)(2,1)} %bitcast.113, bf16[3,4,24,128,128]{4,3,2,1,0:T(8,128)(2,1)} %get-tuple-element.323, s32[]{:T(128)S(6)} %copy.97), kind=kOutput, calls=%fused_computation.1.clone.1 | convolution fusion | flops 1207959552 | bytes 31457284 | tf_op jit(solution)/shard_map/while/body/eval_jaxpr/itab,itubc->ituac/dot_general | solution.py:41
  264.0 18.8 %copy.86 = f32[4,24,3,128,128]{4,1,2,3,0:T(8,128)} copy(f32[4,24,3,128,128]{3,4,2,1,0:T(8,128)} %convolution_bitcast_fusion.6) | data formatting | bytes 37748736 | tf_op jit(solution)/shard_map/while/body/eval_jaxpr/itab,itubc->ituac/transpose | solution.py:41
  282.9 0.1 select_reduce_fusion.4
  283.1 0.1 reduce_sum.29
  283.2 10.5 %fusion.52 = f32[3,4,3,128,128]{4,2,3,1,0:T(4,128)S(1)} fusion(f32[3,4,3,128,128]{4,2,3,1,0:T(4,128)S(1)} %get-tuple-element.310, s32[]{:T(128)S(6)} %copy.97, f32[4,24,3,128,128]{4,1,2,3,0:T(8,128)} %copy.86, s32[4,3]{1,0:T(4,128)S(1)} %get-tuple-element.283, s32[4,24,3]{1,2,0:T(4,128)S(1)} %copy.87, pred[4,24,3]{1,2,0:T(4,128)(4,1)S(1)} %copy.88, ...), kind=kOutput, calls=%fused_computation.6.clone.1 | convolution fusion | flops 169871904 | bytes 19935748 | tf_op jit(solution)/shard_map/while/body/eval_jaxpr/itus,ituac->isac/dot_general | solution.py:44
  293.8 12.5 %fusion.51 = bf16[12,8,384,128]{3,1,2,0:T(8,128)(2,1)} fusion(bf16[192,49152]{1,0:T(8,128)(2,1)} %get-tuple-element.322, s32[96]{0:T(128)S(1)} %eq.133), kind=kOutput, calls=%fused_computation.2.clone.1 | convolution fusion | flops 1816676352 | bytes 28311936 | tf_op jit(solution)/shard_map/while/body/eval_jaxpr/dot_general | solution.py:11
  306.4 10.0 %copy.85 = bf16[12,8,384,128]{3,2,1,0:T(8,128)(2,1)} copy(bf16[12,8,384,128]{3,1,2,0:T(8,128)(2,1)} %fusion.51) | data formatting | bytes 18874368 | tf_op jit(solution)/shard_map/while
  316.4 10.8 %convolution_bitcast_fusion.6 = f32[4,24,3,128,128]{3,4,2,1,0:T(8,128)} fusion(bf16[4,24,3,128,128]{4,3,2,1,0:T(8,128)(2,1)} %bitcast.113, bf16[3,4,24,128,128]{4,3,2,1,0:T(8,128)(2,1)} %get-tuple-element.323, s32[]{:T(128)S(6)} %copy.97), kind=kOutput, calls=%fused_computation.1.clone.1 | convolution fusion | flops 1207959552 | bytes 31457284 | tf_op jit(solution)/shard_map/while/body/eval_jaxpr/itab,itubc->ituac/dot_general | solution.py:41
  327.1 18.8 %copy.86 = f32[4,24,3,128,128]{4,1,2,3,0:T(8,128)} copy(f32[4,24,3,128,128]{3,4,2,1,0:T(8,128)} %convolution_bitcast_fusion.6) | data formatting | bytes 37748736 | tf_op jit(solution)/shard_map/while/body/eval_jaxpr/itab,itubc->ituac/transpose | solution.py:41
  346.0 0.1 select_reduce_fusion.4
  346.2 0.1 reduce_sum.29
  346.3 10.5 %fusion.52 = f32[3,4,3,128,128]{4,2,3,1,0:T(4,128)S(1)} fusion(f32[3,4,3,128,128]{4,2,3,1,0:T(4,128)S(1)} %get-tuple-element.310, s32[]{:T(128)S(6)} %copy.97, f32[4,24,3,128,128]{4,1,2,3,0:T(8,128)} %copy.86, s32[4,3]{1,0:T(4,128)S(1)} %get-tuple-element.283, s32[4,24,3]{1,2,0:T(4,128)S(1)} %copy.87, pred[4,24,3]{1,2,0:T(4,128)(4,1)S(1)} %copy.88, ...), kind=kOutput, calls=%fused_computation.6.clone.1 | convolution fusion | flops 169871904 | bytes 19935748 | tf_op jit(solution)/shard_map/while/body/eval_jaxpr/itus,ituac->isac/dot_general | solution.py:44
  356.8 0.6 convert_element_type.27
  357.5 1.4 copy.63
  358.9 53.8 %all-gather.5.cloned.1.call-done = bf16[12,24,128,128]{3,2,1,0:T(8,128)(2,1)} async-done(((bf16[12,3,128,128]{3,2,1,0:T(8,128)(2,1)}), bf16[12,24,128,128]{3,2,1,0:T(8,128)(2,1)}) %all-gather.5.cloned.1.call-update) | async-done | bytes 9437200 | tf_op jit(solution)/shard_map/all_gather | solution.py:77
  412.7 2.3 broadcast.126
  415.0 192.2 %while.21 = (s32[]{:T(128)}, f32[3,4,3,128,128]{4,2,3,1,0:T(4,128)}, s32[3,4,24]{2,1,0:T(4,128)S(1)}, s32[192,3]{0,1:T(4,128)S(1)}, s32[3,4,3]{2,1,0:T(4,128)S(1...) while((s32[]{:T(128)}, f32[3,4,3,128,128]{4,2,3,1,0:T(4,128)}, ...), condition=%wide.region_5.6_spmd, body=%wide.region_3.5_spmd.sunk | while | flops 3194637056 | bytes 136367200 | solution.py:46
  415.0 0.1 eq.143
  415.1 12.7 %fusion.58 = bf16[12,8,384,128]{3,1,2,0:T(8,128)(2,1)} fusion(bf16[192,49152]{1,0:T(8,128)(2,1)} %get-tuple-element.346, s32[96]{0:T(128)S(1)} %eq.143), kind=kOutput, calls=%fused_computation.26.clone.1 | convolution fusion | flops 1816676352 | bytes 28311936 | tf_op jit(solution)/shard_map/while/body/eval_jaxpr/dot_general | solution.py:11
  427.8 10.1 %copy.89 = bf16[12,8,384,128]{3,2,1,0:T(8,128)(2,1)} copy(bf16[12,8,384,128]{3,1,2,0:T(8,128)(2,1)} %fusion.58) | data formatting | bytes 18874368 | tf_op jit(solution)/shard_map/while
  437.8 10.6 %convolution_bitcast_fusion.7 = f32[4,24,3,128,128]{3,4,2,1,0:T(8,128)} fusion(bf16[4,24,3,128,128]{4,3,2,1,0:T(8,128)(2,1)} %bitcast.114, bf16[3,4,24,128,128]{4,3,2,1,0:T(8,128)(2,1)} %get-tuple-element.347, s32[]{:T(128)S(6)} %copy.103), kind=kOutput, calls=%fused_computation.25.clone.1 | convolution fusion | flops 1207959552 | bytes 31457284 | tf_op jit(solution)/shard_map/while/body/eval_jaxpr/itab,itubc->ituac/dot_general | solution.py:41
  448.5 18.8 %copy.90 = f32[4,24,3,128,128]{4,1,2,3,0:T(8,128)} copy(f32[4,24,3,128,128]{3,4,2,1,0:T(8,128)} %convolution_bitcast_fusion.7) | data formatting | bytes 37748736 | tf_op jit(solution)/shard_map/while/body/eval_jaxpr/itab,itubc->ituac/transpose | solution.py:41
  467.4 0.1 select_reduce_fusion.5
  467.5 0.1 reduce_sum.31
  467.6 11.4 %fusion.59 = f32[3,4,3,128,128]{4,2,3,1,0:T(4,128)} fusion(f32[3,4,3,128,128]{4,2,3,1,0:T(4,128)} %get-tuple-element.334, s32[]{:T(128)S(6)} %copy.103, f32[4,24,3,128,128]{4,1,2,3,0:T(8,128)} %copy.90, s32[4,3]{1,0:T(4,128)S(1)} %get-tuple-element.296, s32[4,24,3]{1,2,0:T(4,128)S(1)} %copy.91, pred[4,24,3]{1,2,0:T(4,128)(4,1)S(1)} %copy.92, ...), kind=kOutput, calls=%fused_computation.30.clone.1 | convolution fusion | flops 169871904 | bytes 19924448 | tf_op jit(solution)/shard_map/while/body/eval_jaxpr/itus,ituac->isac/dot_general | solution.py:44
  479.2 12.7 %fusion.58 = bf16[12,8,384,128]{3,1,2,0:T(8,128)(2,1)} fusion(bf16[192,49152]{1,0:T(8,128)(2,1)} %get-tuple-element.346, s32[96]{0:T(128)S(1)} %eq.143), kind=kOutput, calls=%fused_computation.26.clone.1 | convolution fusion | flops 1816676352 | bytes 28311936 | tf_op jit(solution)/shard_map/while/body/eval_jaxpr/dot_general | solution.py:11
  491.9 10.1 %copy.89 = bf16[12,8,384,128]{3,2,1,0:T(8,128)(2,1)} copy(bf16[12,8,384,128]{3,1,2,0:T(8,128)(2,1)} %fusion.58) | data formatting | bytes 18874368 | tf_op jit(solution)/shard_map/while
  501.9 10.6 %convolution_bitcast_fusion.7 = f32[4,24,3,128,128]{3,4,2,1,0:T(8,128)} fusion(bf16[4,24,3,128,128]{4,3,2,1,0:T(8,128)(2,1)} %bitcast.114, bf16[3,4,24,128,128]{4,3,2,1,0:T(8,128)(2,1)} %get-tuple-element.347, s32[]{:T(128)S(6)} %copy.103), kind=kOutput, calls=%fused_computation.25.clone.1 | convolution fusion | flops 1207959552 | bytes 31457284 | tf_op jit(solution)/shard_map/while/body/eval_jaxpr/itab,itubc->ituac/dot_general | solution.py:41
  512.6 18.8 %copy.90 = f32[4,24,3,128,128]{4,1,2,3,0:T(8,128)} copy(f32[4,24,3,128,128]{3,4,2,1,0:T(8,128)} %convolution_bitcast_fusion.7) | data formatting | bytes 37748736 | tf_op jit(solution)/shard_map/while/body/eval_jaxpr/itab,itubc->ituac/transpose | solution.py:41
  531.5 0.1 select_reduce_fusion.5
  531.6 0.1 reduce_sum.31
  531.7 11.4 %fusion.59 = f32[3,4,3,128,128]{4,2,3,1,0:T(4,128)} fusion(f32[3,4,3,128,128]{4,2,3,1,0:T(4,128)} %get-tuple-element.334, s32[]{:T(128)S(6)} %copy.103, f32[4,24,3,128,128]{4,1,2,3,0:T(8,128)} %copy.90, s32[4,3]{1,0:T(4,128)S(1)} %get-tuple-element.296, s32[4,24,3]{1,2,0:T(4,128)S(1)} %copy.91, pred[4,24,3]{1,2,0:T(4,128)(4,1)S(1)} %copy.92, ...), kind=kOutput, calls=%fused_computation.30.clone.1 | convolution fusion | flops 169871904 | bytes 19924448 | tf_op jit(solution)/shard_map/while/body/eval_jaxpr/itus,ituac->isac/dot_general | solution.py:44
  543.2 12.7 %fusion.58 = bf16[12,8,384,128]{3,1,2,0:T(8,128)(2,1)} fusion(bf16[192,49152]{1,0:T(8,128)(2,1)} %get-tuple-element.346, s32[96]{0:T(128)S(1)} %eq.143), kind=kOutput, calls=%fused_computation.26.clone.1 | convolution fusion | flops 1816676352 | bytes 28311936 | tf_op jit(solution)/shard_map/while/body/eval_jaxpr/dot_general | solution.py:11
  555.9 10.1 %copy.89 = bf16[12,8,384,128]{3,2,1,0:T(8,128)(2,1)} copy(bf16[12,8,384,128]{3,1,2,0:T(8,128)(2,1)} %fusion.58) | data formatting | bytes 18874368 | tf_op jit(solution)/shard_map/while
  566.0 10.6 %convolution_bitcast_fusion.7 = f32[4,24,3,128,128]{3,4,2,1,0:T(8,128)} fusion(bf16[4,24,3,128,128]{4,3,2,1,0:T(8,128)(2,1)} %bitcast.114, bf16[3,4,24,128,128]{4,3,2,1,0:T(8,128)(2,1)} %get-tuple-element.347, s32[]{:T(128)S(6)} %copy.103), kind=kOutput, calls=%fused_computation.25.clone.1 | convolution fusion | flops 1207959552 | bytes 31457284 | tf_op jit(solution)/shard_map/while/body/eval_jaxpr/itab,itubc->ituac/dot_general | solution.py:41
  576.6 18.8 %copy.90 = f32[4,24,3,128,128]{4,1,2,3,0:T(8,128)} copy(f32[4,24,3,128,128]{3,4,2,1,0:T(8,128)} %convolution_bitcast_fusion.7) | data formatting | bytes 37748736 | tf_op jit(solution)/shard_map/while/body/eval_jaxpr/itab,itubc->ituac/transpose | solution.py:41
  595.5 0.1 select_reduce_fusion.5
  595.7 0.1 reduce_sum.31
  595.8 11.4 %fusion.59 = f32[3,4,3,128,128]{4,2,3,1,0:T(4,128)} fusion(f32[3,4,3,128,128]{4,2,3,1,0:T(4,128)} %get-tuple-element.334, s32[]{:T(128)S(6)} %copy.103, f32[4,24,3,128,128]{4,1,2,3,0:T(8,128)} %copy.90, s32[4,3]{1,0:T(4,128)S(1)} %get-tuple-element.296, s32[4,24,3]{1,2,0:T(4,128)S(1)} %copy.91, pred[4,24,3]{1,2,0:T(4,128)(4,1)S(1)} %copy.92, ...), kind=kOutput, calls=%fused_computation.30.clone.1 | convolution fusion | flops 169871904 | bytes 19924448 | tf_op jit(solution)/shard_map/while/body/eval_jaxpr/itus,ituac->isac/dot_general | solution.py:44
  607.2 4.1 subtract_convert_fusion
  611.3 1.3 copy.65
  (47 shorter events, 1.0 us)
Async XLA Ops:
  6.5 136.0 %all-gather.3.cloned.1.call-start = ((), (), s32[]{:S(2)}) async-start(), calls=%async_computation | async-start | bytes 20054016 | tf_op jit(solution)/shard_map/all_gather | solution.py:71
  17.8 394.9 %all-gather.5.cloned.1.call-start = ((), (), s32[]{:S(2)}) async-start(), calls=%async_computation.1 | async-start | bytes 10616832 | tf_op jit(solution)/shard_map/all_gather | solution.py:77
  356.8 58.2 %copy-start = (f32[3,4,3,128,128]{4,2,3,1,0:T(4,128)}, f32[3,4,3,128,128]{4,2,3,1,0:T(4,128)S(1)}, u32[]{:S(2)}) copy-start(f32[3,4,3,128,128]{4,2,3,1,0:T(4,128)S(1)} %get-tuple-element.79) | copy-start | bytes 7077892
Sparse Core Ops, SparseCore 0:
  17.9 124.5 all-gather.2
  359.0 53.6 all-gather.4
where the time goes:
time: 624 us; the launch traced here: 619 us
  local copies, waits for them, and re-layouts  209 us (33%)
  matrix products  206 us (33%)
  waiting for transfers between devices  177 us (28%)
  other arithmetic  14.2 us (2%)
  between operations  13.5 us (2%)
    all_gather x1, waiting for transfers between devices, local(): lax.all_gather(own_tile.reshape(tile_cells, block_size, block_size), 'row...  123 us
    transpose x6, local copies, waits for them, and re-layouts, one_group(): jnp.einsum('itab,itubc->ituac', left_group, picked, preferred_element_typ...  113 us
    dot_general x6, matrix products, pick_rows(): jnp.dot(onehot.astype(jnp.bfloat16), panel_flat, preferred_element_type=j...  75.7 us
    dot_general x6, matrix products, one_group(): jnp.einsum('itus,ituac->isac', weights, products, precision=lax.Precision...  65.8 us
    dot_general x6, matrix products, one_group(): jnp.einsum('itab,itubc->ituac', left_group, picked, preferred_element_typ...  64.1 us
    while x6, local copies, waits for them, and re-layouts  60.2 us
    all_gather x1, waiting for transfers between devices, local(): square_band = lax.all_gather(square_half, 'col', axis=1, tiled=True)  53.8 us
    another operation x1, local copies, waits for them, and re-layouts, contract(): panel.reshape(block_rows, group_slots * block_size * block_size)  24.5 us
  transfers between devices with their start and end apart: 2, of which 2 were waited for; matrix products, arithmetic and copies ran while one was open for 0% of the time, Pallas kernels for 0%

commit v1 on v0

v1 whole, which is shorter than its diff:
```python
import functools
import math

import jax
import jax.numpy as jnp
from jax import lax
from jax.experimental import pallas as pl
from jax.experimental.pallas import tpu as pltpu
from jax.sharding import PartitionSpec as P

F32 = jnp.float32
BF16 = jnp.bfloat16
I32 = jnp.int32
CAP1 = 40
CAP2 = 48
JOB = 1024
MESH = pl.DeviceIdType.MESH


def fdiv(x, n):
    return jnp.floor((x + 0.5) * (1.0 / n))


def mm(a, b, contract=((1,), (0,))):
    return lax.dot_general(
        a.astype(BF16), b.astype(BF16), (contract, ((), ())), preferred_element_type=F32
    )


NT = ((1,), (1,))


def ones_where(cond):
    return jnp.where(cond, 1.0, 0.0).astype(F32)


def plan_body(rc_ref, cols_ref, src1_ref, src2_ref, jobs_ref, flag_ref, own_ref, *, dims):
    side, band_rows, width, per = dims
    count, slots = cols_ref.shape
    row_here, col_here = rc_ref[0], rc_ref[1]
    odd = lax.rem(col_here, 2)
    hi_here = row_here // side
    lo_here = lax.rem(row_here, side)
    p_here = jnp.where(odd == 0, lo_here, hi_here)
    q_here = jnp.where(odd == 0, hi_here, lo_here)
    odd_f = odd.astype(F32)
    p_f, q_f = p_here.astype(F32), q_here.astype(F32)

    square = (count, count)
    row_at = lax.broadcasted_iota(I32, square, 0).astype(F32)
    lane_at = lax.broadcasted_iota(I32, square, 1).astype(F32)
    group = fdiv(lane_at, width)

    def coords(index):
        band = fdiv(index, band_rows)
        hi = fdiv(band, side)
        lo = band - side * hi
        p = odd_f * hi + (1.0 - odd_f) * lo
        q = odd_f * lo + (1.0 - odd_f) * hi
        p = p - p_f
        q = q - q_f
        return band, p + side * ones_where(p < 0.0), q + side * ones_where(q < 0.0)

    band, prel, qrel = coords(row_at)
    band_lane, _, qrel_lane = coords(lane_at)
    own_row = row_at - band_rows * band

    slot_row = lax.broadcasted_iota(I32, (slots, count), 0).astype(F32)
    slot_lane = lax.broadcasted_iota(I32, (slots, count), 1).astype(F32)
    cols = cols_ref[...].astype(F32)
    occupied = jnp.zeros(square, F32)
    slot = per * group
    for u in range(per):
        expand = ones_where(slot_row == per * fdiv(slot_lane, width) + u)
        hit = ones_where(mm(cols, expand) == lane_at)
        occupied = occupied + hit
        slot = slot + u * hit
    own_ref[...] = jnp.where(occupied > 0.0, slot, -1.0)

    in_group = ones_where(group == col_here.astype(F32))
    part = occupied * in_group
    shared = mm(part, part, NT)
    wanted = occupied * jnp.maximum(in_group, ones_where(shared > 0.0))
    identity = ones_where(row_at == lane_at)
    flipped = mm(identity, occupied, NT)
    wanted_b = wanted.astype(BF16)

    def needed_by(d, e):
        pd, qe = lax.rem(p_here + d, side), lax.rem(q_here + e, side)
        who = jnp.where(odd == 0, qe * side + pd, pd * side + qe).astype(F32)
        picked = flipped * ones_where(band_lane == who)
        return occupied * ones_where(mm(picked, wanted_b) > 0.0)

    before = ones_where(row_at < lane_at)
    in_band = ones_where((lane_at < row_at) & (band_lane == band))
    in_class = ones_where((lane_at < row_at) & (qrel_lane == qrel))
    everything = jnp.ones(square, BF16)

    def rank_of(need, earlier):
        return mm(need, before) + mm(mm(earlier, need), everything)

    class_row = lax.broadcasted_iota(I32, (8, count), 0).astype(F32)
    _, _, class_of = coords(lax.broadcasted_iota(I32, (8, count), 1).astype(F32))
    classes = ones_where(class_of == class_row)
    most1 = jnp.zeros((1, count), F32)
    most2 = jnp.zeros((8, 1), F32)
    union, direct = [], []
    for d in range(side):
        total = None
        for e in range(side):
            need = needed_by(d, e)
            sums = jnp.sum(mm(classes, need), axis=1, keepdims=True)
            sums = sums * ones_where(class_row[:, :1] != float(e))
            most2 = jnp.maximum(most2, sums)
            total = need if total is None else jnp.maximum(total, need)
            if d == 0:
                direct.append(need)
        union.append(total)
    rank1, rank2 = [], []
    for d in range(side):
        rank = rank_of(union[d], in_band)
        rank1.append(rank)
        used = (rank + 1.0) * union[d] * ones_where(prel != float(d))
        most1 = jnp.maximum(most1, jnp.max(used, axis=0, keepdims=True))
        rank2.append(rank_of(direct[d], in_class))
    over1 = jnp.max(most1, axis=1, keepdims=True) > float(CAP1)
    over2 = jnp.max(most2, axis=0, keepdims=True) > float(CAP2)
    over = jnp.where(over1 | over2, 1, 0).astype(I32)
    flag_ref[...] = jnp.broadcast_to(over, flag_ref.shape)

    def invert(rank, value_hi, value_lo, cap):
        rows = []
        value = 64.0 * value_hi + value_lo
        for n in range(cap):
            rows.append(jnp.sum(jnp.where(rank == float(n + 1), value, 0.0), axis=0, keepdims=True))
        return jnp.concatenate(rows, axis=0)

    def to_lanes(stack):
        ones = jnp.ones((8, stack.shape[1]), F32)
        return lax.dot_general(
            ones, stack, (NT, ((), ())), preferred_element_type=F32, precision=lax.Precision.HIGHEST
        )

    sel_row = lax.broadcasted_iota(I32, (16, count), 0).astype(F32)
    sel_lane = lax.broadcasted_iota(I32, (16, count), 1).astype(F32)
    first = (row_here * band_rows).astype(F32)
    pick = ones_where((sel_lane == sel_row + first) & (sel_row < float(band_rows)))
    slot16 = mm(pick, slot)
    place = sel_row * slots + slot16
    zeros16 = jnp.zeros_like(place)
    stacks = []
    for d in range(1, side):
        rank = mm(pick, jnp.minimum((rank1[d] + 1.0) * union[d], 255.0))
        stacks.append(invert(rank, zeros16, place, CAP1))
    src1 = to_lanes(jnp.concatenate(stacks, axis=0))
    src1_ref[...] = src1.astype(I32)

    in_recv1 = (prel - 1.0) * CAP1 + jnp.minimum(rank1[0], CAP1 - 1.0)
    in_band_at = own_row * slots + slot
    after1 = jnp.where(prel == 0.0, (side - 1.0) * CAP1 + in_band_at, in_recv1)
    members = side * band_rows
    mem_row = lax.broadcasted_iota(I32, (members, count), 0).astype(F32)
    mem_lane = lax.broadcasted_iota(I32, (members, count), 1).astype(F32)
    mem_band, mem_p, mem_q = coords(mem_lane)
    pick = ones_where(
        (mem_q == 0.0) & (mem_p * band_rows + (mem_lane - band_rows * mem_band) == mem_row)
    )
    after_hi = fdiv(after1, 64)
    hi48 = mm(pick, after_hi)
    lo48 = mm(pick, after1 - 64.0 * after_hi)
    stacks = []
    for e in range(1, side):
        rank = mm(pick, jnp.minimum((rank2[e] + 1.0) * direct[e], 255.0))
        stacks.append(invert(rank, hi48, lo48, CAP2))
    src2 = to_lanes(jnp.concatenate(stacks, axis=0))
    src2_ref[...] = src2.astype(I32)

    held = band_rows * slots
    loc = jnp.where(
        prel + qrel == 0.0,
        in_band_at,
        jnp.where(
            qrel == 0.0,
            held + in_recv1,
            held + (side - 1.0) * CAP1 + (qrel - 1.0) * CAP2 + jnp.minimum(rank2[0], CAP2 - 1.0),
        ),
    )
    loc_hi = fdiv(loc, 64)
    loc_lo = (loc - 64.0 * loc_hi).astype(BF16)
    loc_hi = loc_hi.astype(BF16)
    occ_b = occupied.astype(BF16)
    small = (slots, count)
    t_at = lax.broadcasted_iota(I32, small, 0).astype(F32)
    wide_at = lax.broadcasted_iota(I32, (128, count), 0).astype(F32)
    pack = 4
    wide_i = fdiv(wide_at, 128 // pack)
    wide_t = wide_at - (128 // pack) * wide_i
    tri = ones_where(
        lax.broadcasted_iota(I32, (slots, slots), 1) < lax.broadcasted_iota(I32, (slots, slots), 0)
    )
    t_out = lax.broadcasted_iota(I32, (slots, 128), 0).astype(F32)
    wanted_rows = mm(jnp.where(sel_row + first == sel_lane, 1.0, 0.0), wanted)
    for g in range(band_rows // pack):
        exists = jnp.zeros((slots, 128), F32)
        at_hi = jnp.zeros((slots, 128), F32)
        at_lo = jnp.zeros((slots, 128), F32)
        for ii in range(pack):
            i = g * pack + ii
            line = own_ref[pl.ds(row_here * band_rows + i, 1), :]
            left = ones_where(t_at == line).astype(BF16)
            right = ones_where((wide_i == float(ii)) & (wide_t == line))
            right = (right * wanted_rows[i : i + 1, :]).astype(BF16)
            exists = exists + mm(mm(left, occ_b), right, NT)
            at_hi = at_hi + mm(mm(left, loc_hi), right, NT)
            at_lo = at_lo + mm(mm(left, loc_lo), right, NT)
        rank = jnp.where(exists > 0.0, mm(tri, exists), -1.0)
        code = t_out * JOB + at_hi * 64.0 + at_lo
        rows = []
        for n in range(slots):
            rows.append(jnp.sum(jnp.where(rank == float(n), code, 0.0), axis=0, keepdims=True))
        rows.append(jnp.sum(exists, axis=0, keepdims=True))
        flags = jnp.zeros((1, 128), F32)
        for ii in range(pack):
            i = g * pack + ii
            line = own_ref[pl.ds(row_here * band_rows + i, 1), :]
            right = ones_where((wide_i == float(ii)) & (wide_t == line)).astype(BF16)
            mark = jnp.broadcast_to(wanted_rows[i : i + 1, :], (8, count))
            flags = flags + mm(mark, right, NT)[:1]
        rows.append(flags)
        rows.append(jnp.zeros((32 - slots - 2, 128), F32))
        jobs_ref[g] = jnp.concatenate(rows, axis=0).astype(I32)


def make_plan(rc, cols, dims):
    side, band_rows, _, _ = dims
    count = cols.shape[0]
    groups = band_rows // 4
    return pl.pallas_call(
        functools.partial(plan_body, dims=dims),
        out_shape=(
            jax.ShapeDtypeStruct((8, (side - 1) * CAP1), I32),
            jax.ShapeDtypeStruct((8, (side - 1) * CAP2), I32),
            jax.ShapeDtypeStruct((groups, 32, 128), I32),
            jax.ShapeDtypeStruct((8, 128), I32),
        ),
        in_specs=[
            pl.BlockSpec(memory_space=pltpu.SMEM),
            pl.BlockSpec(memory_space=pltpu.VMEM),
        ],
        out_specs=[pl.BlockSpec(memory_space=pltpu.VMEM)] * 4,
        scratch_shapes=[pltpu.VMEM((count, count), F32)],
        name="plan",
    )(rc, cols)


def gather_body(index_ref, *refs, sizes):
    sources, out_ref, sem = refs[: len(sizes)], refs[len(sizes)], refs[-1]
    total = out_ref.shape[0]

    def issue(n, carry):
        at = index_ref[0, n]
        start = 0
        for ref, size in zip(sources, sizes):
            inside = (at >= start) & (at < start + size)

            @pl.when(inside)
            def _(ref=ref, start=start):
                pltpu.make_async_copy(ref.at[at - start], out_ref.at[n], sem).start()

            start += size
        return carry

    lax.fori_loop(0, total, issue, 0, unroll=4)
    pltpu.make_async_copy(out_ref, out_ref, sem).wait()


def gather(index, total, *sources):
    block = sources[0].shape[1:]
    return pl.pallas_call(
        functools.partial(gather_body, sizes=tuple(s.shape[0] for s in sources)),
        out_shape=jax.ShapeDtypeStruct((total, *block), sources[0].dtype),
        in_specs=[pl.BlockSpec(memory_space=pltpu.SMEM)]
        + [pl.BlockSpec(memory_space=pl.ANY)] * len(sources),
        out_specs=pl.BlockSpec(memory_space=pltpu.VMEM),
        scratch_shapes=[pltpu.SemaphoreType.DMA],
        name="gather",
    )(index, *sources)


def ring_body(*refs, side, cols, stage, flags):
    if flags:
        send_ref, flag_ref, recv_ref, heard_ref = refs[:4]
    else:
        send_ref, recv_ref = refs[:2]
    relay_up, relay_down, send_sem, recv_sem = refs[-4:]
    row, col = lax.axis_index("row"), lax.axis_index("col")
    hi, lo = row // side, lax.rem(row, side)
    low_axis = lax.rem(col + stage, 2)

    def along(d):
        by_lo = hi * side + lax.rem(lo + d, side)
        by_hi = lax.rem(hi + d, side) * side + lo
        return (by_lo * (1 - low_axis) + by_hi * low_axis, col)

    right, left = along(1), along(side - 1)
    peers = [(row, lax.rem(col + k, cols)) for k in range(1, cols)] if flags else []
    barrier = pltpu.get_barrier_semaphore()
    for peer in [right, left, *peers]:
        pl.semaphore_signal(barrier, inc=1, device_id=peer, device_id_type=MESH)
    pl.semaphore_wait(barrier, 2 + len(peers))

    half = send_ref.shape[1] // 2
    lower, upper = pl.ds(0, half), pl.ds(half, half)

    def copy(n, src, dst, peer):
        return pltpu.make_async_remote_copy(
            src_ref=src,
            dst_ref=dst,
            send_sem=send_sem.at[n],
            recv_sem=recv_sem.at[n],
            device_id=peer,
            device_id_type=MESH,
        )

    far_up = copy(0, send_ref.at[1, lower], relay_up, right)
    far_down = copy(1, send_ref.at[1, upper], relay_down, left)
    near_up = copy(2, send_ref.at[0], recv_ref.at[2], right)
    near_down = copy(3, send_ref.at[2], recv_ref.at[0], left)
    next_up = copy(4, relay_up, recv_ref.at[1, lower], right)
    next_down = copy(5, relay_down, recv_ref.at[1, upper], left)
    told = [copy(6 + k, flag_ref, heard_ref.at[k], peer) for k, peer in enumerate(peers)]
    far_up.start()
    far_down.start()
    near_up.start()
    near_down.start()
    for one in told:
        one.start()
    far_up.wait_recv()
    next_up.start()
    far_down.wait_recv()
    next_down.start()
    far_up.wait_send()
    far_down.wait_send()
    for one in told:
        one.wait()
    near_up.wait()
    near_down.wait()
    next_up.wait()
    next_down.wait()


def ring(send, flag, side, cols, stage):
    three, cap, *block = send.shape
    flags = flag is not None
    copies = 6 + (cols - 1 if flags else 0)
    out_shape = [jax.ShapeDtypeStruct(send.shape, send.dtype)]
    if flags:
        out_shape.append(jax.ShapeDtypeStruct((cols - 1, *flag.shape), flag.dtype))
    return pl.pallas_call(
        functools.partial(ring_body, side=side, cols=cols, stage=stage, flags=flags),
        out_shape=out_shape,
        in_specs=[pl.BlockSpec(memory_space=pl.ANY)] * (2 if flags else 1),
        out_specs=[pl.BlockSpec(memory_space=pl.ANY)] * len(out_shape),
        scratch_shapes=[
            pltpu.VMEM((cap // 2, *block), send.dtype),
            pltpu.VMEM((cap // 2, *block), send.dtype),
            pltpu.SemaphoreType.DMA((copies,)),
            pltpu.SemaphoreType.DMA((copies,)),
        ],
        compiler_params=pltpu.CompilerParams(collective_id=stage, has_side_effects=True),
        name="ring",
    )(*([send, flag] if flags else [send]))


def products_body(rc_ref, jobs_ref, band_ref, recv1_ref, recv2_ref, out_ref, held, half, square, sem, *, per):
    n_band, n1, n2 = band_ref.shape[0], recv1_ref.shape[0], recv2_ref.shape[0]
    copies = [
        pltpu.make_async_copy(band_ref, held.at[pl.ds(0, n_band)], sem.at[0]),
        pltpu.make_async_copy(recv1_ref, held.at[pl.ds(n_band, n1)], sem.at[1]),
        pltpu.make_async_copy(recv2_ref, held.at[pl.ds(n_band + n1, n2)], sem.at[2]),
    ]
    for one in copies:
        one.start()
    col_here = rc_ref[1]
    rows = out_ref.shape[0]
    slots = n_band // rows
    block = out_ref.shape[2:]
    for one in copies:
        one.wait()

    def job(i, t):
        return i // 4, lax.rem(i, 4) * 32 + t

    def summed(left, i, t):
        g, lane = job(i, t)

        def step(q, acc):
            code = jobs_ref[g, q, lane]
            at = lax.rem(code, JOB)
            return acc + jnp.dot(
                left[i * slots + code // JOB], held[at], preferred_element_type=F32
            )

        return lax.fori_loop(0, jobs_ref[g, slots, lane], step, jnp.zeros(block, F32))

    def first(n, carry):
        i, t = n // slots, lax.rem(n, slots)
        g, lane = job(i, t)

        @pl.when(jobs_ref[g, slots + 1, lane] > 0)
        def _():
            total = summed(held, i, t)
            half[n] = total.astype(BF16)
            s = t - col_here * per

            @pl.when((s >= 0) & (s < per))
            def _():
                square[i * per + s] = total

        return carry

    lax.fori_loop(0, n_band, first, 0)

    def second(n, carry):
        i, s = n // per, lax.rem(n, per)
        t = col_here * per + s
        g, lane = job(i, t)
        wanted = jobs_ref[g, slots + 1, lane] > 0

        @pl.when(wanted)
        def _():
            cube = summed(half, i, t)
            out_ref[i, s] = (3.0 * square[n] - 2.0 * cube).astype(BF16)

        @pl.when(jnp.logical_not(wanted))
        def _():
            out_ref[i, s] = jnp.zeros(block, BF16)

        return carry

    lax.fori_loop(0, rows * per, second, 0)


def products(rc, jobs, band, recv1, recv2, rows, per):
    block = band.shape[1:]
    return pl.pallas_call(
        functools.partial(products_body, per=per),
        out_shape=jax.ShapeDtypeStruct((rows, per, *block), BF16),
        in_specs=[pl.BlockSpec(memory_space=pltpu.SMEM)] * 2
        + [pl.BlockSpec(memory_space=pl.ANY)] * 3,
        out_specs=pl.BlockSpec(memory_space=pltpu.VMEM),
        scratch_shapes=[
            pltpu.VMEM((band.shape[0] + recv1.shape[0] + recv2.shape[0], *block), BF16),
            pltpu.VMEM(band.shape, BF16),
            pltpu.VMEM((rows * per, *block), F32),
            pltpu.SemaphoreType.DMA((3,)),
        ],
        compiler_params=pltpu.CompilerParams(vmem_limit_bytes=60 * 1024 * 1024),
        name="products",
    )(rc, jobs, band, recv1, recv2)


def spread_body(x_ref, out_ref, send_sem, recv_sem, *, axis, size):
    row, col = lax.axis_index("row"), lax.axis_index("col")

    def peer(k):
        if axis == "row":
            return (lax.rem(row + k, size), col)
        return (row, lax.rem(col + k, size))

    barrier = pltpu.get_barrier_semaphore()
    for k in range(1, size):
        pl.semaphore_signal(barrier, inc=1, device_id=peer(k), device_id_type=MESH)
    pl.semaphore_wait(barrier, size - 1)
    copies = []
    for k in range(1, size):
        one = pltpu.make_async_remote_copy(
            src_ref=x_ref,
            dst_ref=out_ref.at[k - 1],
            send_sem=send_sem.at[k - 1],
            recv_sem=recv_sem.at[k - 1],
            device_id=peer(k),
            device_id_type=MESH,
        )
        one.start()
        copies.append(one)
    for one in copies:
        one.wait()


def spread(x, axis, size, collective_id):
    others = pl.pallas_call(
        functools.partial(spread_body, axis=axis, size=size),
        out_shape=jax.ShapeDtypeStruct((size - 1, *x.shape), x.dtype),
        in_specs=[pl.BlockSpec(memory_space=pl.ANY)],
        out_specs=pl.BlockSpec(memory_space=pl.ANY),
        scratch_shapes=[pltpu.SemaphoreType.DMA((size - 1,)), pltpu.SemaphoreType.DMA((size - 1,))],
        compiler_params=pltpu.CompilerParams(collective_id=collective_id, has_side_effects=True),
        name="spread",
    )(x)
    return jnp.concatenate([x[None], others], axis=0)


def dense_body(rc_ref, cols_ref, left_ref, panel_ref, out_ref, left, right, acc, sem, *, dims, mixed):
    side, band_rows, _, per = dims
    slots = cols_ref.shape[1]
    row_here, col_here = rc_ref[0], rc_ref[1]
    tile = band_rows * per
    row_count, col_count = side * side, slots // per

    def one_out(n, carry):
        i, s = n // per, lax.rem(n, per)
        target = cols_ref[row_here * band_rows + i, col_here * per + s]
        acc[...] = jnp.zeros_like(acc)

        def one_t(t, carry):
            k = cols_ref[row_here * band_rows + i, t]
            safe = jnp.maximum(k, 0)
            away = lax.rem(row_here - safe // band_rows + row_count, row_count)
            if mixed:
                back = lax.rem(col_here - t // per + col_count, col_count)
                at_left = back * tile + i * per + lax.rem(t, per)
            else:
                at_left = i * slots + t
            for u in range(per):
                found = cols_ref[safe, col_here * per + u]

                @pl.when((k >= 0) & (target >= 0) & (found == target))
                def _(u=u):
                    at = away * tile + lax.rem(safe, band_rows) * per + u
                    a = pltpu.make_async_copy(left_ref.at[at_left], left, sem.at[0])
                    b = pltpu.make_async_copy(panel_ref.at[at], right, sem.at[1])
                    a.start()
                    b.start()
                    a.wait()
                    b.wait()
                    acc[...] += jnp.dot(left[...], right[...], preferred_element_type=F32)

            return carry

        lax.fori_loop(0, slots, one_t, 0)
        out_ref[n] = acc[...]
        return carry

    lax.fori_loop(0, tile, one_out, 0)


def dense_step(rc, cols, left, panel, dims, mixed):
    _, band_rows, _, per = dims
    block = left.shape[1:]
    return pl.pallas_call(
        functools.partial(dense_body, dims=dims, mixed=mixed),
        out_shape=jax.ShapeDtypeStruct((band_rows * per, *block), F32),
        in_specs=[pl.BlockSpec(memory_space=pltpu.SMEM)] * 2
        + [pl.BlockSpec(memory_space=pl.ANY)] * 2,
        out_specs=pl.BlockSpec(memory_space=pltpu.VMEM),
        scratch_shapes=[
            pltpu.VMEM(block, BF16),
            pltpu.VMEM(block, BF16),
            pltpu.VMEM(block, F32),
            pltpu.SemaphoreType.DMA((2,)),
        ],
        name="dense_step",
    )(rc, cols, left, panel)


def dense(rc, cols, density, dims, sizes):
    _, band_rows, _, per = dims
    rows, slots, *block = density.shape
    row_size, col_size = sizes
    tile = lax.dynamic_slice_in_dim(density, rc[1] * per, per, 1)
    tile = tile.reshape(band_rows * per, *block)
    panel = spread(tile, "row", row_size, 2).reshape(-1, *block)
    square = dense_step(rc, cols, density.reshape(-1, *block), panel, dims, False)
    half = spread(square.astype(BF16), "col", col_size, 3).reshape(-1, *block)
    cube = dense_step(rc, cols, half, panel, dims, True)
    return (3.0 * square - 2.0 * cube).astype(BF16).reshape(rows, per, *block)


def local(density, cols, *, sizes):
    rows, slots, *block = density.shape
    row_size, col_size = sizes
    side = math.isqrt(row_size)
    per = slots // col_size
    width = cols.shape[0] // col_size
    dims = (side, rows, width, per)
    rc = jnp.stack([lax.axis_index("row"), lax.axis_index("col")]).astype(I32)
    band = density.reshape(rows * slots, *block)
    src1, src2, jobs, flag = make_plan(rc, cols, dims)
    near = (side - 1) * CAP1
    far = (side - 1) * CAP2
    packed = gather(src1, near, band)
    recv1, heard = ring(packed.reshape(side - 1, CAP1, *block), flag, side, col_size, 0)
    recv1 = recv1.reshape(near, *block)
    packed = gather(src2, far, recv1, band)
    (recv2,) = ring(packed.reshape(side - 1, CAP2, *block), None, side, col_size, 1)
    recv2 = recv2.reshape(far, *block)
    over = jnp.max(heard) + flag[0, 0] > 0
    return lax.cond(
        over,
        lambda: dense(rc, cols, density, dims, sizes),
        lambda: products(rc, jobs, band, recv1, recv2, rows, per),
    )


def solution(mesh):
    sizes = (mesh.shape["row"], mesh.shape["col"])
    return jax.shard_map(
        functools.partial(local, sizes=sizes),
        mesh=mesh,
        in_specs=(P("row", None, None, None), P()),
        out_specs=P("row", "col", None, None),
        check_vma=False,
    )
```

time: 624 us -> 147 us (0.24)
  the two profiles are of different devices: /device:TPU:0 before, /device:TPU:54 now
where the time goes in v1:
time: 147 us
  Pallas kernels  141 us (96%)
  local copies, waits for them, and re-layouts  2.7 us (2%)
  other arithmetic  1.47 us (1%)
    pallas_call x2, Pallas kernels, ring(): pl.pallas_call(functools.partial(ring_body, side=side, cols=cols, stage=s...  73.6 us
    pallas_call x1, Pallas kernels, products(): pl.pallas_call(functools.partial(products_body, per=per), out_shape=jax.S...  43.6 us
    pallas_call x2, Pallas kernels, gather(): pl.pallas_call(functools.partial(gather_body, sizes=tuple((s.shape[0] for...  14.4 us
    pallas_call x1, Pallas kernels, make_plan(): pl.pallas_call(functools.partial(plan_body, dims=dims), out_shape=(jax.Sh...  9.8 us

profile of v1, /device:TPU:54, one launch (start us, length us, event | category | flops | bytes accessed | tf_op | source)
XLA Modules:
  0.0 146.9 jit_solution(11718591563056765739)
XLA Ops:
  0.0 0.1 pad_add_fusion.rc_ref
  0.1 1.5 %copy.5.cols_ref = s32[192,24]{1,0:T(8,128)} copy(s32[192,24]{0,1:T(8,128)} %param.5) | data formatting | bytes 36864 | tf_op args[1]
  1.6 9.8 %plan.1 = (s32[8,120]{1,0:T(8,128)}, s32[8,144]{1,0:T(8,128)}, s32[3,32,128]{2,1,0:T(8,128)S(1)}, s32[8,128]{1,0:T(8,128)}) custom-call(s32[2]{0:T(128)S(1)} %pad_add_fusion.rc_ref, s32[192,24]{1,0:T(8,128)} %copy.5.cols_ref), custom_call_target="tpu_custom_call" | custom-call | tf_op jit(solution)/shard_map/plan/pallas_call | solution.py:238
  11.3 1.2 slice.3
  12.6 6.3 %gather.2 = bf16[120,128,128]{2,1,0:T(8,128)(2,1)} custom-call(s32[8,120]{1,0:T(8,128)} %get-tuple-element.42.index_ref, bf16[288,128,128]{2,1,0:T(8,128)(2,1)} %bitcast.18), custom_call_target="tpu_custom_call" | custom-call | tf_op jit(solution)/shard_map/gather/pallas_call | solution.py:279
  18.9 33.5 %ring.2 = (bf16[3,40,128,128]{3,2,1,0:T(8,128)(2,1)}, s32[7,8,128]{2,1,0:T(8,128)}) custom-call(bf16[3,40,128,128]{3,2,1,0:T(8,128)(2,1)} %bitcast.27, s32[8,128]{1,0:T(8,128)} %get-tuple-element.43.refs_1_), custom_call_target="tpu_custom_call" | custom-call | tf_op jit(solution)/shard_map/ring/pallas_call | solution.py:359
  52.4 1.4 reduce_max.9
  55.0 8.2 %gather.3 = bf16[144,128,128]{2,1,0:T(8,128)(2,1)} custom-call(s32[8,144]{1,0:T(8,128)} %get-tuple-element.45.index_ref, bf16[120,128,128]{2,1,0:T(8,128)(2,1)} %bitcast.25, bf16[288,128,128]{2,1,0:T(8,128)(2,1)} %bitcast.19), custom_call_target="tpu_custom_call" | custom-call | tf_op jit(solution)/shard_map/gather/pallas_call | solution.py:279
  63.2 0.0 copy-start.2
  63.2 40.1 %ring.3 = bf16[3,48,128,128]{3,2,1,0:T(8,128)(2,1)} custom-call(bf16[3,48,128,128]{3,2,1,0:T(8,128)(2,1)} %bitcast.24), custom_call_target="tpu_custom_call" | custom-call | tf_op jit(solution)/shard_map/ring/pallas_call | solution.py:359
  103.3 0.0 copy-done.2
  103.3 43.6 %conditional.1 = (bf16[12,3,128,128]{3,2,1,0:T(8,128)(2,1)}) conditional(s32[]{:T(128)} %convert_element_type.9, (bf16[3,48,128,128]{3,2,1,0:T(8,128)(2,1)}, s32[2]{0:T(128)S(1)}, s32[3,32,128]{2,1,0:T(8,128)S(1)}, bf16[288,128,128]{2,1,0:T(8,128)(2,1)}, bf16[120,128,128]{2,1,0:T(8,128)(2,1)}) %tuple.19, (bf16[12,24,128,128]{3,2,1,0:T(8,128)(2,1)}, ...), branch_computations={%region_1.0_spmd, %region_2.0_spmd} | conditional | flops 17694724 | bytes 86151288 | solution.py:599
  103.3 43.6 %products.1 = bf16[12,3,128,128]{3,2,1,0:T(8,128)(2,1)} custom-call(s32[2]{0:T(128)S(1)} %get-tuple-element.27.rc_ref, s32[3,32,128]{2,1,0:T(8,128)S(1)} %get-tuple-element.28.jobs_ref, bf16[288,128,128]{2,1,0:T(8,128)(2,1)} %get-tuple-element.29.band_ref, bf16[120,128,128]{2,1,0:T(8,128)(2,1)} %get-tuple-element.30.recv1_ref, bf16[144,128,128]{2,1,0:T(8,128)(2,1)} %bitcast.23), custom_call_target="tpu_custom_call" | custom-call | tf_op jit(solution)/shard_map/cond/branch_0_fun/products/pallas_call | solution.py:446
Async XLA Ops:
  63.2 40.1 %copy-start.2 = (s32[192,24]{0,1:T(8,128)S(1)}, s32[192,24]{0,1:T(8,128)}, u32[]{:S(2)}) copy-start(s32[192,24]{0,1:T(8,128)} %param.5) | copy-start | bytes 55300

commit v2 on v1

--- a/solution.py
+++ b/solution.py
@@ -130,7 +130,7 @@
 
     def invert(rank, value_hi, value_lo, cap):
         rows = []
-        value = 64.0 * value_hi + value_lo
+        value = 64.0 * value_hi + value_lo + 1.0
         for n in range(cap):
             rows.append(jnp.sum(jnp.where(rank == float(n + 1), value, 0.0), axis=0, keepdims=True))
         return jnp.concatenate(rows, axis=0)
@@ -257,8 +257,8 @@
     sources, out_ref, sem = refs[: len(sizes)], refs[len(sizes)], refs[-1]
     total = out_ref.shape[0]
 
-    def issue(n, carry):
-        at = index_ref[0, n]
+    def issue(n, count):
+        at = index_ref[0, n] - 1
         start = 0
         for ref, size in zip(sources, sizes):
             inside = (at >= start) & (at < start + size)
@@ -268,10 +268,15 @@
                 pltpu.make_async_copy(ref.at[at - start], out_ref.at[n], sem).start()
 
             start += size
+        return count + jnp.where(at >= 0, 1, 0)
+
+    count = lax.fori_loop(0, total, issue, jnp.zeros((), I32), unroll=4)
+
+    def settle(n, carry):
+        pltpu.make_async_copy(out_ref.at[0], out_ref.at[0], sem).wait()
         return carry
 
-    lax.fori_loop(0, total, issue, 0, unroll=4)
-    pltpu.make_async_copy(out_ref, out_ref, sem).wait()
+    lax.fori_loop(0, count, settle, 0)
 
 
 def gather(index, total, *sources):
@@ -372,7 +377,9 @@
     )(*([send, flag] if flags else [send]))
 
 
-def products_body(rc_ref, jobs_ref, band_ref, recv1_ref, recv2_ref, out_ref, held, half, square, sem, *, per):
+def products_body(
+    rc_ref, jobs_ref, band_ref, recv1_ref, recv2_ref, out_ref, held, half, square, cube, todo, extra, sem, *, per
+):
     n_band, n1, n2 = band_ref.shape[0], recv1_ref.shape[0], recv2_ref.shape[0]
     copies = [
         pltpu.make_async_copy(band_ref, held.at[pl.ds(0, n_band)], sem.at[0]),
@@ -381,68 +388,128 @@
     ]
     for one in copies:
         one.start()
-    col_here = rc_ref[1]
     rows = out_ref.shape[0]
+    tile = rows * per
     slots = n_band // rows
     block = out_ref.shape[2:]
+    blank = n_band + n1 + n2
+    first_own = rc_ref[1] * per
+    held[blank] = jnp.zeros(block, BF16)
+    half[n_band] = jnp.zeros(block, BF16)
+
+    def listed(i, t, number, own_at, count, more, left_blank):
+        g, lane = i // 4, lax.rem(i, 4) * 32 + t
+        n = jobs_ref[g, slots, lane]
+        todo[0, count] = number
+        todo[1, count] = own_at
+        for q in range(2):
+            code = jobs_ref[g, q, lane]
+            there = n > q
+            todo[2 + 2 * q, count] = jnp.where(there, i * slots + code // JOB, left_blank)
+            todo[3 + 2 * q, count] = jnp.where(there, lax.rem(code, JOB), blank)
+        extra[0, more] = number
+        extra[1, more] = own_at
+        extra[2, more] = i
+        extra[3, more] = t
+        return count + 1, more + jnp.where(n > 2, 1, 0)
+
+    def plan_row(i, carry):
+        def plan_one(t, carry):
+            count, more = carry
+            g, lane = i // 4, lax.rem(i, 4) * 32 + t
+            s = t - first_own
+            own = (s >= 0) & (s < per)
+            wanted = (jobs_ref[g, slots + 1, lane] > 0) | own
+            own_at = jnp.where(own, i * per + s, tile)
+            after, extra_after = listed(i, t, i * slots + t, own_at, count, more, blank)
+            return jnp.where(wanted, after, count), jnp.where(wanted, extra_after, more)
+
+        return lax.fori_loop(0, slots, plan_one, carry)
+
+    zero = jnp.zeros((), I32)
+    count, more = lax.fori_loop(0, rows, plan_row, (zero, zero))
+
+    def pad(k, carry):
+        todo[0, count + k] = n_band
+        todo[1, count + k] = tile
+        for q in range(2, 6):
+            todo[q, count + k] = blank
+        return carry
+
+    lax.fori_loop(0, 3, pad, 0)
     for one in copies:
         one.wait()
 
-    def job(i, t):
-        return i // 4, lax.rem(i, 4) * 32 + t
-
-    def summed(left, i, t):
-        g, lane = job(i, t)
+    def pair(left, m):
+        a = jnp.concatenate([left[todo[2, m]], left[todo[4, m]]], axis=1)
+        b = jnp.concatenate([held[todo[3, m]], held[todo[5, m]]], axis=0)
+        return jnp.dot(a, b, preferred_element_type=F32)
+
+    def rest(left, i, t, acc):
+        g, lane = i // 4, lax.rem(i, 4) * 32 + t
 
         def step(q, acc):
             code = jobs_ref[g, q, lane]
-            at = lax.rem(code, JOB)
-            return acc + jnp.dot(
-                left[i * slots + code // JOB], held[at], preferred_element_type=F32
-            )
-
-        return lax.fori_loop(0, jobs_ref[g, slots, lane], step, jnp.zeros(block, F32))
-
-    def first(n, carry):
-        i, t = n // slots, lax.rem(n, slots)
-        g, lane = job(i, t)
-
-        @pl.when(jobs_ref[g, slots + 1, lane] > 0)
-        def _():
-            total = summed(held, i, t)
-            half[n] = total.astype(BF16)
-            s = t - col_here * per
-
-            @pl.when((s >= 0) & (s < per))
-            def _():
-                square[i * per + s] = total
-
+            a = left[i * slots + code // JOB]
+            return acc + jnp.dot(a, held[lax.rem(code, JOB)], preferred_element_type=F32)
+
+        return lax.fori_loop(2, jobs_ref[g, slots, lane], step, acc)
+
+    def four(m4, carry):
+        sums = [pair(held, m4 * 4 + k) for k in range(4)]
+        for k in range(4):
+            half[todo[0, m4 * 4 + k]] = sums[k].astype(BF16)
+        for k in range(4):
+            square[todo[1, m4 * 4 + k]] = sums[k]
         return carry
 
-    lax.fori_loop(0, n_band, first, 0)
-
-    def second(n, carry):
+    lax.fori_loop(0, (count + 3) // 4, four, 0)
+
+    def late(m, carry):
+        i, t = extra[2, m], extra[3, m]
+        code0, code1 = jobs_ref[i // 4, 0, lax.rem(i, 4) * 32 + t], jobs_ref[i // 4, 1, lax.rem(i, 4) * 32 + t]
+        acc = jnp.dot(held[i * slots + code0 // JOB], held[lax.rem(code0, JOB)], preferred_element_type=F32)
+        acc = acc + jnp.dot(
+            held[i * slots + code1 // JOB], held[lax.rem(code1, JOB)], preferred_element_type=F32
+        )
+        acc = rest(held, i, t, acc)
+        half[extra[0, m]] = acc.astype(BF16)
+        square[extra[1, m]] = acc
+        return carry
+
+    lax.fori_loop(0, more, late, 0)
+
+    def plan_cube(n, more):
         i, s = n // per, lax.rem(n, per)
-        t = col_here * per + s
-        g, lane = job(i, t)
-        wanted = jobs_ref[g, slots + 1, lane] > 0
-
-        @pl.when(wanted)
-        def _():
-            cube = summed(half, i, t)
-            out_ref[i, s] = (3.0 * square[n] - 2.0 * cube).astype(BF16)
-
-        @pl.when(jnp.logical_not(wanted))
-        def _():
-            out_ref[i, s] = jnp.zeros(block, BF16)
-
+        _, after = listed(i, first_own + s, n, n, n, more, n_band)
+        return after
+
+    more = lax.fori_loop(0, tile, plan_cube, zero)
+
+    def four_cubes(m4, carry):
+        sums = [pair(half, m4 * 4 + k) for k in range(4)]
+        for k in range(4):
+            cube[m4 * 4 + k] = sums[k]
         return carry
 
-    lax.fori_loop(0, rows * per, second, 0)
+    lax.fori_loop(0, tile // 4, four_cubes, 0)
+
+    def late_cube(m, carry):
+        n = extra[0, m]
+        cube[n] = rest(half, extra[2, m], extra[3, m], cube[n])
+        return carry
+
+    lax.fori_loop(0, more, late_cube, 0)
+    for i in range(rows):
+        for s in range(per):
+            n = i * per + s
+            out_ref[i, s] = (3.0 * square[n] - 2.0 * cube[n]).astype(BF16)
 
 
 def products(rc, jobs, band, recv1, recv2, rows, per):
     block = band.shape[1:]
+    blocks = band.shape[0] + recv1.shape[0] + recv2.shape[0]
+    lists = band.shape[0] + 8
     return pl.pallas_call(
         functools.partial(products_body, per=per),
         out_shape=jax.ShapeDtypeStruct((rows, per, *block), BF16),
@@ -450,9 +517,12 @@
         + [pl.BlockSpec(memory_space=pl.ANY)] * 3,
         out_specs=pl.BlockSpec(memory_space=pltpu.VMEM),
         scratch_shapes=[
-            pltpu.VMEM((band.shape[0] + recv1.shape[0] + recv2.shape[0], *block), BF16),
-            pltpu.VMEM(band.shape, BF16),
+            pltpu.VMEM((blocks + 1, *block), BF16),
+            pltpu.VMEM((band.shape[0] + 1, *block), BF16),
+            pltpu.VMEM((rows * per + 1, *block), F32),
             pltpu.VMEM((rows * per, *block), F32),
+            pltpu.SMEM((6, lists), I32),
+            pltpu.SMEM((4, lists), I32),
             pltpu.SemaphoreType.DMA((3,)),
         ],
         compiler_params=pltpu.CompilerParams(vmem_limit_bytes=60 * 1024 * 1024),

time: 147 us -> 130 us (0.88)
  the two profiles are of different devices: /device:TPU:54 before, /device:TPU:0 now
where the time goes in v2:
time: 130 us
  Pallas kernels  124 us (95%)
  local copies, waits for them, and re-layouts  2.7 us (2%)
  other arithmetic  1.47 us (1%)
  between operations  1.31 us (1%)
    pallas_call x2, Pallas kernels, ring(): pl.pallas_call(functools.partial(ring_body, side=side, cols=cols, stage=s...  76.6 us
    pallas_call x1, Pallas kernels, products(): pl.pallas_call(functools.partial(products_body, per=per), out_shape=jax.S...  28.5 us
    pallas_call x1, Pallas kernels, make_plan(): pl.pallas_call(functools.partial(plan_body, dims=dims), out_shape=(jax.Sh...  10.1 us
    pallas_call x2, Pallas kernels, gather(): pl.pallas_call(functools.partial(gather_body, sizes=tuple((s.shape[0] for...  8.93 us

profile of v2, /device:TPU:0, one launch (start us, length us, event | category | flops | bytes accessed | tf_op | source)
XLA Modules:
  0.0 129.6 jit_solution(10470000937405895795)
XLA Ops:
  0.0 0.1 pad_add_fusion.rc_ref
  0.1 1.5 %copy.5.cols_ref = s32[192,24]{1,0:T(8,128)} copy(s32[192,24]{0,1:T(8,128)} %param.5) | data formatting | bytes 36864 | tf_op args[1]
  1.6 10.1 %plan.1 = (s32[8,120]{1,0:T(8,128)}, s32[8,144]{1,0:T(8,128)}, s32[3,32,128]{2,1,0:T(8,128)S(1)}, s32[8,128]{1,0:T(8,128)}) custom-call(s32[2]{0:T(128)S(1)} %pad_add_fusion.rc_ref, s32[192,24]{1,0:T(8,128)} %copy.5.cols_ref), custom_call_target="tpu_custom_call" | custom-call | tf_op jit(solution)/shard_map/plan/pallas_call | solution.py:238
  11.6 1.2 slice.3
  12.9 4.2 %gather.2 = bf16[120,128,128]{2,1,0:T(8,128)(2,1)} custom-call(s32[8,120]{1,0:T(8,128)} %get-tuple-element.42.index_ref, bf16[288,128,128]{2,1,0:T(8,128)(2,1)} %bitcast.18), custom_call_target="tpu_custom_call" | custom-call | tf_op jit(solution)/shard_map/gather/pallas_call | solution.py:284
  17.0 36.2 %ring.2 = (bf16[3,40,128,128]{3,2,1,0:T(8,128)(2,1)}, s32[7,8,128]{2,1,0:T(8,128)}) custom-call(bf16[3,40,128,128]{3,2,1,0:T(8,128)(2,1)} %bitcast.27, s32[8,128]{1,0:T(8,128)} %get-tuple-element.43.refs_1_), custom_call_target="tpu_custom_call" | custom-call | tf_op jit(solution)/shard_map/ring/pallas_call | solution.py:364
  53.2 1.4 %reduce_max.9 = s32[]{:T(128)} reduce(s32[7,8,128]{2,1,0:T(8,128)} %get-tuple-element.44, s32[]{:T(128)} %constant.21.clone.1), dimensions={0,1,2}, to_apply=%region_0.0 | reduce | flops 7167 | bytes 28680 | tf_op jit(solution)/shard_map/reduce_max | solution.py:668
  55.9 4.8 %gather.3 = bf16[144,128,128]{2,1,0:T(8,128)(2,1)} custom-call(s32[8,144]{1,0:T(8,128)} %get-tuple-element.45.index_ref, bf16[120,128,128]{2,1,0:T(8,128)(2,1)} %bitcast.25, bf16[288,128,128]{2,1,0:T(8,128)(2,1)} %bitcast.19), custom_call_target="tpu_custom_call" | custom-call | tf_op jit(solution)/shard_map/gather/pallas_call | solution.py:284
  60.7 0.0 copy-start.2
  60.7 40.4 %ring.3 = bf16[3,48,128,128]{3,2,1,0:T(8,128)(2,1)} custom-call(bf16[3,48,128,128]{3,2,1,0:T(8,128)(2,1)} %bitcast.24), custom_call_target="tpu_custom_call" | custom-call | tf_op jit(solution)/shard_map/ring/pallas_call | solution.py:364
  101.0 0.0 copy-done.2
  101.1 28.5 %conditional.1 = (bf16[12,3,128,128]{3,2,1,0:T(8,128)(2,1)}) conditional(s32[]{:T(128)} %convert_element_type.9, (bf16[3,48,128,128]{3,2,1,0:T(8,128)(2,1)}, s32[2]{0:T(128)S(1)}, s32[3,32,128]{2,1,0:T(8,128)S(1)}, bf16[288,128,128]{2,1,0:T(8,128)(2,1)}, bf16[120,128,128]{2,1,0:T(8,128)(2,1)}) %tuple.19, (bf16[12,24,128,128]{3,2,1,0:T(8,128)(2,1)}, ...), branch_computations={%region_1.0_spmd, %region_2.0_spmd} | conditional | flops 17694724 | bytes 86151288 | solution.py:669
  101.1 28.5 %products.1 = bf16[12,3,128,128]{3,2,1,0:T(8,128)(2,1)} custom-call(s32[2]{0:T(128)S(1)} %get-tuple-element.27.rc_ref, s32[3,32,128]{2,1,0:T(8,128)S(1)} %get-tuple-element.28.jobs_ref, bf16[288,128,128]{2,1,0:T(8,128)(2,1)} %get-tuple-element.29.band_ref, bf16[120,128,128]{2,1,0:T(8,128)(2,1)} %get-tuple-element.30.recv1_ref, bf16[144,128,128]{2,1,0:T(8,128)(2,1)} %bitcast.23), custom_call_target="tpu_custom_call" | custom-call | tf_op jit(solution)/shard_map/cond/branch_0_fun/products/pallas_call | solution.py:513
Async XLA Ops:
  60.7 40.4 %copy-start.2 = (s32[192,24]{0,1:T(8,128)S(1)}, s32[192,24]{0,1:T(8,128)}, u32[]{:S(2)}) copy-start(s32[192,24]{0,1:T(8,128)} %param.5) | copy-start | bytes 55300

commit v3 on v1

--- a/solution.py
+++ b/solution.py
@@ -14,6 +14,7 @@
 CAP1 = 40
 CAP2 = 48
 JOB = 1024
+LEVELS = 3
 MESH = pl.DeviceIdType.MESH
 
 
@@ -34,7 +35,7 @@
     return jnp.where(cond, 1.0, 0.0).astype(F32)
 
 
-def plan_body(rc_ref, cols_ref, src1_ref, src2_ref, jobs_ref, flag_ref, own_ref, *, dims):
+def plan_body(rc_ref, cols_ref, src1_ref, src2_ref, jobs_ref, todo_ref, flag_ref, own_ref, *, dims):
     side, band_rows, width, per = dims
     count, slots = cols_ref.shape
     row_here, col_here = rc_ref[0], rc_ref[1]
@@ -130,7 +131,7 @@
 
     def invert(rank, value_hi, value_lo, cap):
         rows = []
-        value = 64.0 * value_hi + value_lo
+        value = 64.0 * value_hi + value_lo + 1.0
         for n in range(cap):
             rows.append(jnp.sum(jnp.where(rank == float(n + 1), value, 0.0), axis=0, keepdims=True))
         return jnp.concatenate(rows, axis=0)
@@ -181,8 +182,8 @@
         in_band_at,
         jnp.where(
             qrel == 0.0,
-            held + in_recv1,
-            held + (side - 1.0) * CAP1 + (qrel - 1.0) * CAP2 + jnp.minimum(rank2[0], CAP2 - 1.0),
+            held + 1.0 + in_recv1,
+            held + 1.0 + (side - 1.0) * CAP1 + (qrel - 1.0) * CAP2 + jnp.minimum(rank2[0], CAP2 - 1.0),
         ),
     )
     loc_hi = fdiv(loc, 64)
@@ -200,10 +201,12 @@
     )
     t_out = lax.broadcasted_iota(I32, (slots, 128), 0).astype(F32)
     wanted_rows = mm(jnp.where(sel_row + first == sel_lane, 1.0, 0.0), wanted)
+    parts = []
     for g in range(band_rows // pack):
         exists = jnp.zeros((slots, 128), F32)
         at_hi = jnp.zeros((slots, 128), F32)
         at_lo = jnp.zeros((slots, 128), F32)
+        flags = jnp.zeros((1, 128), F32)
         for ii in range(pack):
             i = g * pack + ii
             line = own_ref[pl.ds(row_here * band_rows + i, 1), :]
@@ -213,22 +216,70 @@
             exists = exists + mm(mm(left, occ_b), right, NT)
             at_hi = at_hi + mm(mm(left, loc_hi), right, NT)
             at_lo = at_lo + mm(mm(left, loc_lo), right, NT)
+            flags = flags + mm(jnp.ones((8, count), BF16), right, NT)[:1]
         rank = jnp.where(exists > 0.0, mm(tri, exists), -1.0)
         code = t_out * JOB + at_hi * 64.0 + at_lo
         rows = []
         for n in range(slots):
             rows.append(jnp.sum(jnp.where(rank == float(n), code, 0.0), axis=0, keepdims=True))
         rows.append(jnp.sum(exists, axis=0, keepdims=True))
-        flags = jnp.zeros((1, 128), F32)
-        for ii in range(pack):
-            i = g * pack + ii
-            line = own_ref[pl.ds(row_here * band_rows + i, 1), :]
-            right = ones_where((wide_i == float(ii)) & (wide_t == line)).astype(BF16)
-            mark = jnp.broadcast_to(wanted_rows[i : i + 1, :], (8, count))
-            flags = flags + mm(mark, right, NT)[:1]
         rows.append(flags)
-        rows.append(jnp.zeros((32 - slots - 2, 128), F32))
-        jobs_ref[g] = jnp.concatenate(rows, axis=0).astype(I32)
+        parts.append(rows)
+        spare = jnp.zeros((32 - slots - 2, 128), F32)
+        jobs_ref[g] = jnp.concatenate([*rows, spare], axis=0).astype(I32)
+
+    lanes = 128 * len(parts)
+
+    def whole(n):
+        return jnp.concatenate([rows[n] for rows in parts], axis=1)
+
+    at = lax.broadcasted_iota(I32, (1, lanes), 1).astype(F32)
+    i_at = fdiv(at, 128 // pack)
+    t_of = at - (128 // pack) * i_at
+    mine = t_of - per * col_here.astype(F32)
+    own = ones_where((mine >= 0.0) & (mine < per))
+    number_of = i_at * slots + t_of
+    own_at = i_at * per + mine
+    n_of = whole(slots)
+    needed = jnp.maximum(whole(slots + 1), own)
+    upper = ones_where(
+        lax.broadcasted_iota(I32, (lanes, lanes), 0) < lax.broadcasted_iota(I32, (lanes, lanes), 1)
+    ).astype(BF16)
+    place_at = lax.broadcasted_iota(I32, (lanes, lanes), 0).astype(F32)
+    slot_here = lax.broadcasted_iota(I32, (1, lanes), 1).astype(F32)
+    most = jnp.max(n_of, axis=1, keepdims=True)
+
+    def split(value):
+        high = fdiv(value, 64)
+        return [high, value - 64.0 * high]
+
+    blank = float(held)
+    for level in range(LEVELS):
+        codes = [whole(2 * level + q) for q in range(2)]
+        fields = split(number_of) + split(own_at * own)
+        for q in range(2):
+            there = n_of > float(2 * level + q)
+            t_left = fdiv(codes[q], JOB)
+            fields += split(jnp.where(there, i_at * slots + t_left, blank))
+            fields += split(jnp.where(there, codes[q] - JOB * t_left, blank))
+        table = jnp.concatenate(fields + [jnp.zeros((4, lanes), F32)], axis=0)
+        for kind in range(2):
+            mask = own if kind else needed
+            if level > 0:
+                mask = mask * ones_where(n_of > float(2 * level))
+            rank = mm(jnp.broadcast_to(mask, (8, lanes)), upper)[:1]
+            rank = jnp.where(mask > 0.0, rank, -1.0)
+            packed = mm(table, ones_where(place_at == rank), NT)
+            total = jnp.sum(mask, axis=1, keepdims=True)
+            valid = slot_here < total
+            spare = [blank, float(band_rows * per), blank, blank, blank, blank]
+            rows = []
+            for f in range(6):
+                value = packed[2 * f : 2 * f + 1] * 64.0 + packed[2 * f + 1 : 2 * f + 2]
+                rows.append(jnp.where(valid, value, spare[f]))
+            rows.append(jnp.broadcast_to(total, (1, lanes)))
+            rows.append(jnp.broadcast_to(most, (1, lanes)))
+            todo_ref[2 * level + kind] = jnp.concatenate(rows, axis=0).astype(I32)
 
 
 def make_plan(rc, cols, dims):
@@ -241,13 +292,14 @@
             jax.ShapeDtypeStruct((8, (side - 1) * CAP1), I32),
             jax.ShapeDtypeStruct((8, (side - 1) * CAP2), I32),
             jax.ShapeDtypeStruct((groups, 32, 128), I32),
+            jax.ShapeDtypeStruct((2 * LEVELS, 8, 128 * groups), I32),
             jax.ShapeDtypeStruct((8, 128), I32),
         ),
         in_specs=[
             pl.BlockSpec(memory_space=pltpu.SMEM),
             pl.BlockSpec(memory_space=pltpu.VMEM),
         ],
-        out_specs=[pl.BlockSpec(memory_space=pltpu.VMEM)] * 4,
+        out_specs=[pl.BlockSpec(memory_space=pltpu.VMEM)] * 5,
         scratch_shapes=[pltpu.VMEM((count, count), F32)],
         name="plan",
     )(rc, cols)
@@ -257,8 +309,8 @@
     sources, out_ref, sem = refs[: len(sizes)], refs[len(sizes)], refs[-1]
     total = out_ref.shape[0]
 
-    def issue(n, carry):
-        at = index_ref[0, n]
+    def issue(n, count):
+        at = index_ref[0, n] - 1
         start = 0
         for ref, size in zip(sources, sizes):
             inside = (at >= start) & (at < start + size)
@@ -268,10 +320,15 @@
                 pltpu.make_async_copy(ref.at[at - start], out_ref.at[n], sem).start()
 
             start += size
+        return count + jnp.where(at >= 0, 1, 0)
+
+    count = lax.fori_loop(0, total, issue, jnp.zeros((), I32), unroll=4)
+
+    def settle(n, carry):
+        pltpu.make_async_copy(out_ref.at[0], out_ref.at[0], sem).wait()
         return carry
 
-    lax.fori_loop(0, total, issue, 0, unroll=4)
-    pltpu.make_async_copy(out_ref, out_ref, sem).wait()
+    lax.fori_loop(0, count, settle, 0)
 
 
 def gather(index, total, *sources):
@@ -372,92 +429,124 @@
     )(*([send, flag] if flags else [send]))
 
 
-def products_body(rc_ref, jobs_ref, band_ref, recv1_ref, recv2_ref, out_ref, held, half, square, sem, *, per):
+def products_body(
+    rc_ref, todo_ref, jobs_ref, band_ref, recv1_ref, recv2_ref, out_ref, held, half, acc, cube, jobs, sem, *, per
+):
     n_band, n1, n2 = band_ref.shape[0], recv1_ref.shape[0], recv2_ref.shape[0]
     copies = [
+        pltpu.make_async_copy(recv2_ref, held.at[pl.ds(n_band + 1 + n1, n2)], sem.at[2]),
+        pltpu.make_async_copy(recv1_ref, held.at[pl.ds(n_band + 1, n1)], sem.at[1]),
         pltpu.make_async_copy(band_ref, held.at[pl.ds(0, n_band)], sem.at[0]),
-        pltpu.make_async_copy(recv1_ref, held.at[pl.ds(n_band, n1)], sem.at[1]),
-        pltpu.make_async_copy(recv2_ref, held.at[pl.ds(n_band + n1, n2)], sem.at[2]),
     ]
     for one in copies:
         one.start()
-    col_here = rc_ref[1]
     rows = out_ref.shape[0]
+    tile = rows * per
     slots = n_band // rows
     block = out_ref.shape[2:]
+    first_own = rc_ref[1] * per
+    most = todo_ref[0, 7, 0]
+    held[n_band] = jnp.zeros(block, BF16)
+    half[n_band] = jnp.zeros(block, BF16)
+
+    @pl.when(most > 2 * LEVELS)
+    def _():
+        pltpu.sync_copy(jobs_ref, jobs)
+
     for one in copies:
         one.wait()
 
-    def job(i, t):
-        return i // 4, lax.rem(i, 4) * 32 + t
-
-    def summed(left, i, t):
-        g, lane = job(i, t)
-
-        def step(q, acc):
-            code = jobs_ref[g, q, lane]
-            at = lax.rem(code, JOB)
-            return acc + jnp.dot(
-                left[i * slots + code // JOB], held[at], preferred_element_type=F32
-            )
-
-        return lax.fori_loop(0, jobs_ref[g, slots, lane], step, jnp.zeros(block, F32))
-
-    def first(n, carry):
-        i, t = n // slots, lax.rem(n, slots)
-        g, lane = job(i, t)
-
-        @pl.when(jobs_ref[g, slots + 1, lane] > 0)
-        def _():
-            total = summed(held, i, t)
-            half[n] = total.astype(BF16)
-            s = t - col_here * per
-
-            @pl.when((s >= 0) & (s < per))
+    def pair(left, which, m):
+        a = [left[todo_ref[which, 2 + 2 * q, m]] for q in range(2)]
+        b = [held[todo_ref[which, 3 + 2 * q, m]] for q in range(2)]
+        return jnp.dot(
+            jnp.concatenate(a, axis=1), jnp.concatenate(b, axis=0), preferred_element_type=F32
+        )
+
+    def rest(left, i, t, total):
+        g, lane = i // 4, lax.rem(i, 4) * 32 + t
+
+        def step(q, total):
+            code = jobs[g, q, lane]
+            a = left[i * slots + code // JOB]
+            return total + jnp.dot(a, held[lax.rem(code, JOB)], preferred_element_type=F32)
+
+        return lax.fori_loop(2 * LEVELS, jobs[g, slots, lane], step, total)
+
+    for level in range(LEVELS):
+
+        def four(m4, carry, level=level):
+            sums = [pair(held, 2 * level, m4 * 4 + k) for k in range(4)]
+            for k in range(4):
+                at = todo_ref[2 * level, 0, m4 * 4 + k]
+                total = sums[k] if level == 0 else acc[at] + sums[k]
+                acc[at] = total
+                half[at] = total.astype(BF16)
+            return carry
+
+        lax.fori_loop(0, (todo_ref[2 * level, 6, 0] + 3) // 4, four, 0)
+    half[n_band] = jnp.zeros(block, BF16)
+
+    @pl.when(most > 2 * LEVELS)
+    def _():
+        def late(n, carry):
+            i, t = n // slots, lax.rem(n, slots)
+
+            @pl.when(jobs[i // 4, slots, lax.rem(i, 4) * 32 + t] > 2 * LEVELS)
             def _():
-                square[i * per + s] = total
-
-        return carry
-
-    lax.fori_loop(0, n_band, first, 0)
-
-    def second(n, carry):
-        i, s = n // per, lax.rem(n, per)
-        t = col_here * per + s
-        g, lane = job(i, t)
-        wanted = jobs_ref[g, slots + 1, lane] > 0
-
-        @pl.when(wanted)
-        def _():
-            cube = summed(half, i, t)
-            out_ref[i, s] = (3.0 * square[n] - 2.0 * cube).astype(BF16)
-
-        @pl.when(jnp.logical_not(wanted))
-        def _():
-            out_ref[i, s] = jnp.zeros(block, BF16)
-
-        return carry
-
-    lax.fori_loop(0, rows * per, second, 0)
-
-
-def products(rc, jobs, band, recv1, recv2, rows, per):
+                total = rest(held, i, t, acc[n])
+                acc[n] = total
+                half[n] = total.astype(BF16)
+
+            return carry
+
+        lax.fori_loop(0, n_band, late, 0)
+
+    for level in range(LEVELS):
+
+        def four_cubes(m4, carry, level=level):
+            sums = [pair(half, 2 * level + 1, m4 * 4 + k) for k in range(4)]
+            for k in range(4):
+                at = todo_ref[2 * level + 1, 1, m4 * 4 + k]
+                cube[at] = sums[k] if level == 0 else cube[at] + sums[k]
+            return carry
+
+        lax.fori_loop(0, (todo_ref[2 * level + 1, 6, 0] + 3) // 4, four_cubes, 0)
+
+    @pl.when(most > 2 * LEVELS)
+    def _():
+        def late(n, carry):
+            cube[n] = rest(half, n // per, first_own + lax.rem(n, per), cube[n])
+            return carry
+
+        lax.fori_loop(0, tile, late, 0)
+
+    for i in range(rows):
+        for s in range(per):
+            square = acc[i * slots + first_own + s]
+            out_ref[i, s] = (3.0 * square - 2.0 * cube[i * per + s]).astype(BF16)
+
+
+def products(rc, todo, jobs, band, recv1, recv2, rows, per):
     block = band.shape[1:]
+    blocks = band.shape[0] + recv1.shape[0] + recv2.shape[0]
     return pl.pallas_call(
         functools.partial(products_body, per=per),
         out_shape=jax.ShapeDtypeStruct((rows, per, *block), BF16),
         in_specs=[pl.BlockSpec(memory_space=pltpu.SMEM)] * 2
-        + [pl.BlockSpec(memory_space=pl.ANY)] * 3,
+        + [pl.BlockSpec(memory_space=pl.ANY)] * 4,
         out_specs=pl.BlockSpec(memory_space=pltpu.VMEM),
         scratch_shapes=[
-            pltpu.VMEM((band.shape[0] + recv1.shape[0] + recv2.shape[0], *block), BF16),
-            pltpu.VMEM(band.shape, BF16),
-            pltpu.VMEM((rows * per, *block), F32),
+            pltpu.VMEM((blocks + 1, *block), BF16),
+            pltpu.VMEM((band.shape[0] + 1, *block), BF16),
+            pltpu.VMEM((band.shape[0] + 1, *block), F32),
+            pltpu.VMEM((rows * per + 1, *block), F32),
+            pltpu.SMEM(jobs.shape, I32),
             pltpu.SemaphoreType.DMA((3,)),
         ],
         compiler_params=pltpu.CompilerParams(vmem_limit_bytes=60 * 1024 * 1024),
         name="products",
-    )(rc, jobs, band, recv1, recv2)
+    )(rc, todo, jobs, band, recv1, recv2)
 
 
 def spread_body(x_ref, out_ref, send_sem, recv_sem, *, axis, size):
@@ -586,7 +675,7 @@
     dims = (side, rows, width, per)
     rc = jnp.stack([lax.axis_index("row"), lax.axis_index("col")]).astype(I32)
     band = density.reshape(rows * slots, *block)
-    src1, src2, jobs, flag = make_plan(rc, cols, dims)
+    src1, src2, jobs, todo, flag = make_plan(rc, cols, dims)
     near = (side - 1) * CAP1
     far = (side - 1) * CAP2
     packed = gather(src1, near, band)
@@ -599,7 +688,7 @@
     return lax.cond(
         over,
         lambda: dense(rc, cols, density, dims, sizes),
-        lambda: products(rc, jobs, band, recv1, recv2, rows, per),
+        lambda: products(rc, todo, jobs, band, recv1, recv2, rows, per),
     )
 
 

time: 147 us -> 118 us (0.80)
  the two profiles are of different devices: /device:TPU:54 before, /device:TPU:0 now
where the time goes in v3:
time: 118 us; the launch traced here: 117 us
  Pallas kernels  112 us (95%)
  local copies, waits for them, and re-layouts  2.7 us (2%)
  between operations  1.48 us (1%)
  other arithmetic  1.47 us (1%)
    pallas_call x2, Pallas kernels, ring(): pl.pallas_call(functools.partial(ring_body, side=side, cols=cols, stage=s...  76.6 us
    pallas_call x1, Pallas kernels, products(): pl.pallas_call(functools.partial(products_body, per=per), out_shape=jax.S...  15 us
    pallas_call x1, Pallas kernels, make_plan(): pl.pallas_call(functools.partial(plan_body, dims=dims), out_shape=(jax.Sh...  11.4 us
    pallas_call x2, Pallas kernels, gather(): pl.pallas_call(functools.partial(gather_body, sizes=tuple((s.shape[0] for...  8.62 us

profile of v3, /device:TPU:0, one launch (start us, length us, event | category | flops | bytes accessed | tf_op | source)
XLA Modules:
  0.0 117.5 jit_solution(10991618928866044543)
XLA Ops:
  0.0 0.1 pad_add_fusion.rc_ref
  0.1 1.5 %copy.5.cols_ref = s32[192,24]{1,0:T(8,128)} copy(s32[192,24]{0,1:T(8,128)} %param.5) | data formatting | bytes 36864 | tf_op args[1]
  1.6 11.4 %plan.1 = (s32[8,120]{1,0:T(8,128)}, s32[8,144]{1,0:T(8,128)}, s32[3,32,128]{2,1,0:T(8,128)S(1)}, s32[6,8,384]{2,1,0:T(8,128)S(1)}, s32[8,128]{1,0:T(8,128)}) custom-call(s32[2]{0:T(128)S(1)} %pad_add_fusion.rc_ref, s32[192,24]{1,0:T(8,128)} %copy.5.cols_ref), custom_call_target="tpu_custom_call" | custom-call | tf_op jit(solution)/shard_map/plan/pallas_call | solution.py:289
  12.9 1.2 %slice.3 = s32[1,1]{1,0:T(1,128)} slice(s32[8,128]{1,0:T(8,128)} %get-tuple-element.47.refs_1_), slice={[0:1], [0:1]} | slice | bytes 8 | tf_op jit(solution)/shard_map/slice | solution.py:687
  14.2 3.9 %gather.2 = bf16[120,128,128]{2,1,0:T(8,128)(2,1)} custom-call(s32[8,120]{1,0:T(8,128)} %get-tuple-element.46.index_ref, bf16[288,128,128]{2,1,0:T(8,128)(2,1)} %bitcast.18), custom_call_target="tpu_custom_call" | custom-call | tf_op jit(solution)/shard_map/gather/pallas_call | solution.py:336
  18.1 36.4 %ring.2 = (bf16[3,40,128,128]{3,2,1,0:T(8,128)(2,1)}, s32[7,8,128]{2,1,0:T(8,128)}) custom-call(bf16[3,40,128,128]{3,2,1,0:T(8,128)(2,1)} %bitcast.27, s32[8,128]{1,0:T(8,128)} %get-tuple-element.47.refs_1_), custom_call_target="tpu_custom_call" | custom-call | tf_op jit(solution)/shard_map/ring/pallas_call | solution.py:416
  54.4 1.4 %reduce_max.9 = s32[]{:T(128)} reduce(s32[7,8,128]{2,1,0:T(8,128)} %get-tuple-element.48, s32[]{:T(128)} %constant.21.clone.1), dimensions={0,1,2}, to_apply=%region_0.0 | reduce | flops 7167 | bytes 28680 | tf_op jit(solution)/shard_map/reduce_max | solution.py:687
  57.1 4.7 %gather.3 = bf16[144,128,128]{2,1,0:T(8,128)(2,1)} custom-call(s32[8,144]{1,0:T(8,128)} %get-tuple-element.49.index_ref, bf16[120,128,128]{2,1,0:T(8,128)(2,1)} %bitcast.25, bf16[288,128,128]{2,1,0:T(8,128)(2,1)} %bitcast.19), custom_call_target="tpu_custom_call" | custom-call | tf_op jit(solution)/shard_map/gather/pallas_call | solution.py:336
  61.8 0.0 copy-start.2
  61.8 40.3 %ring.3 = bf16[3,48,128,128]{3,2,1,0:T(8,128)(2,1)} custom-call(bf16[3,48,128,128]{3,2,1,0:T(8,128)(2,1)} %bitcast.24), custom_call_target="tpu_custom_call" | custom-call | tf_op jit(solution)/shard_map/ring/pallas_call | solution.py:416
  102.1 0.0 copy-done.2
  102.1 15.2 %conditional.1 = (bf16[12,3,128,128]{3,2,1,0:T(8,128)(2,1)}) conditional(s32[]{:T(128)} %convert_element_type.9, (bf16[3,48,128,128]{3,2,1,0:T(8,128)(2,1)}, s32[2]{0:T(128)S(1)}, s32[6,8,384]{2,1,0:T(8,128)S(1)}, s32[3,32,128]{2,1,0:T(8,128)S(1)}, bf16[288,128,128]{2,1,0:T(8,128)(2,1)}, /*index=5*/bf16[120,128,128]{2,1,0:T(8,128)(2,1)}) %tuple.19, ...), branch_computations={%region_1.0_spmd, %region_2.0_spmd} | conditional | flops 17694724 | bytes 86151288 | solution.py:688
  102.1 15.0 %products.1 = bf16[12,3,128,128]{3,2,1,0:T(8,128)(2,1)} custom-call(s32[2]{0:T(128)S(1)} %get-tuple-element.29.rc_ref, s32[6,8,384]{2,1,0:T(8,128)S(1)} %get-tuple-element.30.todo_ref, s32[3,32,128]{2,1,0:T(8,128)S(1)} %get-tuple-element.31.jobs_ref, bf16[288,128,128]{2,1,0:T(8,128)(2,1)} %get-tuple-element.32.band_ref, ...), custom_call_target="tpu_custom_call" | custom-call | tf_op jit(solution)/shard_map/cond/branch_0_fun/products/pallas_call | solution.py:533
Async XLA Ops:
  61.8 40.3 %copy-start.2 = (s32[192,24]{0,1:T(8,128)S(1)}, s32[192,24]{0,1:T(8,128)}, u32[]{:S(2)}) copy-start(s32[192,24]{0,1:T(8,128)} %param.5) | copy-start | bytes 55300

commit v4 on v3

--- a/solution.py
+++ b/solution.py
@@ -14,7 +14,9 @@
 CAP1 = 40
 CAP2 = 48
 JOB = 1024
-LEVELS = 3
+LEVELS = 4
+STEPS1 = (26, 30, 34, CAP1)
+STEPS2 = (32, 36, 40, CAP2)
 MESH = pl.DeviceIdType.MESH
 
 
@@ -35,13 +37,14 @@
     return jnp.where(cond, 1.0, 0.0).astype(F32)
 
 
-def plan_body(rc_ref, cols_ref, src1_ref, src2_ref, jobs_ref, todo_ref, flag_ref, own_ref, *, dims):
+def plan_core(
+    row_here, col_here, cols_ref, src1_ref, src2_ref, jobs_ref, todo_ref, own_ref, want_ref, part_ref, counted, *, dims
+):
     side, band_rows, width, per = dims
     count, slots = cols_ref.shape
-    row_here, col_here = rc_ref[0], rc_ref[1]
-    odd = lax.rem(col_here, 2)
     hi_here = row_here // side
     lo_here = lax.rem(row_here, side)
+    odd = lax.rem(col_here, 2)
     p_here = jnp.where(odd == 0, lo_here, hi_here)
     q_here = jnp.where(odd == 0, hi_here, lo_here)
     odd_f = odd.astype(F32)
@@ -85,6 +88,7 @@
     identity = ones_where(row_at == lane_at)
     flipped = mm(identity, occupied, NT)
     wanted_b = wanted.astype(BF16)
+    want_ref[...] = wanted
 
     def needed_by(d, e):
         pd, qe = lax.rem(p_here + d, side), lax.rem(q_here + e, side)
@@ -124,10 +128,16 @@
         used = (rank + 1.0) * union[d] * ones_where(prel != float(d))
         most1 = jnp.maximum(most1, jnp.max(used, axis=0, keepdims=True))
         rank2.append(rank_of(direct[d], in_class))
-    over1 = jnp.max(most1, axis=1, keepdims=True) > float(CAP1)
-    over2 = jnp.max(most2, axis=0, keepdims=True) > float(CAP2)
-    over = jnp.where(over1 | over2, 1, 0).astype(I32)
-    flag_ref[...] = jnp.broadcast_to(over, flag_ref.shape)
+    most1 = jnp.max(most1, axis=1, keepdims=True)
+    most2 = jnp.max(most2, axis=0, keepdims=True)
+    after_counts = counted(most1, most2)
+
+    def tally(need, where):
+        kept = jnp.sum(need * where, axis=0, keepdims=True)
+        return jnp.sum(kept, axis=1, keepdims=True)
+
+    tallies = [tally(union[0], ones_where((qrel == 0.0) & (prel == float(d)))) for d in range(1, side)]
+    tallies += [tally(direct[0], ones_where(qrel == float(e))) for e in range(1, side)]
 
     def invert(rank, value_hi, value_lo, cap):
         rows = []
@@ -200,19 +210,17 @@
         lax.broadcasted_iota(I32, (slots, slots), 1) < lax.broadcasted_iota(I32, (slots, slots), 0)
     )
     t_out = lax.broadcasted_iota(I32, (slots, 128), 0).astype(F32)
-    wanted_rows = mm(jnp.where(sel_row + first == sel_lane, 1.0, 0.0), wanted)
-    parts = []
-    for g in range(band_rows // pack):
+    def one_part(g, carry):
         exists = jnp.zeros((slots, 128), F32)
         at_hi = jnp.zeros((slots, 128), F32)
         at_lo = jnp.zeros((slots, 128), F32)
         flags = jnp.zeros((1, 128), F32)
         for ii in range(pack):
-            i = g * pack + ii
-            line = own_ref[pl.ds(row_here * band_rows + i, 1), :]
+            at_row = row_here * band_rows + g * pack + ii
+            line = own_ref[pl.ds(at_row, 1), :]
             left = ones_where(t_at == line).astype(BF16)
             right = ones_where((wide_i == float(ii)) & (wide_t == line))
-            right = (right * wanted_rows[i : i + 1, :]).astype(BF16)
+            right = (right * want_ref[pl.ds(at_row, 1), :]).astype(BF16)
             exists = exists + mm(mm(left, occ_b), right, NT)
             at_hi = at_hi + mm(mm(left, loc_hi), right, NT)
             at_lo = at_lo + mm(mm(left, loc_lo), right, NT)
@@ -224,14 +232,21 @@
             rows.append(jnp.sum(jnp.where(rank == float(n), code, 0.0), axis=0, keepdims=True))
         rows.append(jnp.sum(exists, axis=0, keepdims=True))
         rows.append(flags)
-        parts.append(rows)
         spare = jnp.zeros((32 - slots - 2, 128), F32)
-        jobs_ref[g] = jnp.concatenate([*rows, spare], axis=0).astype(I32)
-
-    lanes = 128 * len(parts)
+        part_ref[g] = jnp.concatenate([*rows, spare], axis=0)
+        jobs_ref[g] = part_ref[g].astype(I32)
+        return carry
+
+    groups = band_rows // pack
+    lax.fori_loop(0, groups, one_part, 0)
+    if after_counts is not None:
+        after_counts()
+
+    lanes = 128 * groups
+    parts = [part_ref[g] for g in range(groups)]
 
     def whole(n):
-        return jnp.concatenate([rows[n] for rows in parts], axis=1)
+        return jnp.concatenate([rows[n : n + 1] for rows in parts], axis=1)
 
     at = lax.broadcasted_iota(I32, (1, lanes), 1).astype(F32)
     i_at = fdiv(at, 128 // pack)
@@ -278,31 +293,119 @@
                 value = packed[2 * f : 2 * f + 1] * 64.0 + packed[2 * f + 1 : 2 * f + 2]
                 rows.append(jnp.where(valid, value, spare[f]))
             rows.append(jnp.broadcast_to(total, (1, lanes)))
-            rows.append(jnp.broadcast_to(most, (1, lanes)))
+            facts = jnp.broadcast_to(most, (1, lanes))
+            for k, value in enumerate(tallies):
+                facts = jnp.where(slot_here == float(k + 1), value, facts)
+            rows.append(facts)
             todo_ref[2 * level + kind] = jnp.concatenate(rows, axis=0).astype(I32)
 
 
-def make_plan(rc, cols, dims):
+def plan_body(
+    cols_ref,
+    src1_ref,
+    src2_ref,
+    jobs_ref,
+    todo_ref,
+    over_ref,
+    step1_ref,
+    step2_ref,
+    own_ref,
+    want_ref,
+    part_ref,
+    flag_ref,
+    heard_ref,
+    send_sem,
+    recv_sem,
+    *,
+    dims,
+    col_size,
+):
+    row, col = lax.axis_index("row"), lax.axis_index("col")
+    peers = [(row, lax.rem(col + k, col_size)) for k in range(1, col_size)]
+    barrier = pltpu.get_barrier_semaphore()
+    for peer in peers:
+        pl.semaphore_signal(barrier, inc=1, device_id=peer, device_id_type=MESH)
+    pl.semaphore_wait(barrier, col_size - 1)
+    told = [
+        pltpu.make_async_remote_copy(
+            src_ref=flag_ref,
+            dst_ref=heard_ref.at[k],
+            send_sem=send_sem.at[k],
+            recv_sem=recv_sem.at[k],
+            device_id=peer,
+            device_id_type=MESH,
+        )
+        for k, peer in enumerate(peers)
+    ]
+
+    def counted(most1, most2):
+        which = lax.broadcasted_iota(I32, flag_ref.shape, 0)
+        flag_ref[...] = jnp.where(which == 0, most1, most2).astype(I32)
+
+        def tell():
+            for one in told:
+                one.start()
+
+        return tell
+
+    plan_core(
+        row, col, cols_ref, src1_ref, src2_ref, jobs_ref, todo_ref, own_ref, want_ref, part_ref, counted, dims=dims
+    )
+    for one in told:
+        one.wait()
+    heard = flag_ref[...]
+    for k in range(col_size - 1):
+        heard = jnp.maximum(heard, heard_ref[k])
+    most1 = jnp.max(heard[0:1])
+    most2 = jnp.max(heard[1:2])
+
+    def step(most, steps):
+        return sum((most > n).astype(I32) for n in steps[:-1])
+
+    over_ref[0] = ((most1 > STEPS1[-1]) | (most2 > STEPS2[-1])).astype(I32)
+    step1_ref[0] = step(most1, STEPS1)
+    step2_ref[0] = step(most2, STEPS2)
+
+
+def plan_shapes(dims):
     side, band_rows, _, _ = dims
-    count = cols.shape[0]
     groups = band_rows // 4
+    return (
+        jax.ShapeDtypeStruct((8, (side - 1) * CAP1), I32),
+        jax.ShapeDtypeStruct((8, (side - 1) * CAP2), I32),
+        jax.ShapeDtypeStruct((groups, 32, 128), I32),
+        jax.ShapeDtypeStruct((2 * LEVELS, 8, 128 * groups), I32),
+    )
+
+
+def plan_scratch(dims, count):
+    groups = dims[1] // 4
+    return [
+        pltpu.VMEM((count, count), F32),
+        pltpu.VMEM((count, count), F32),
+        pltpu.VMEM((groups, 32, 128), F32),
+    ]
+
+
+def make_plan(cols, dims, col_size):
+    lists = plan_shapes(dims)
+    choice = jax.ShapeDtypeStruct((1,), I32)
     return pl.pallas_call(
-        functools.partial(plan_body, dims=dims),
-        out_shape=(
-            jax.ShapeDtypeStruct((8, (side - 1) * CAP1), I32),
-            jax.ShapeDtypeStruct((8, (side - 1) * CAP2), I32),
-            jax.ShapeDtypeStruct((groups, 32, 128), I32),
-            jax.ShapeDtypeStruct((2 * LEVELS, 8, 128 * groups), I32),
-            jax.ShapeDtypeStruct((8, 128), I32),
-        ),
-        in_specs=[
-            pl.BlockSpec(memory_space=pltpu.SMEM),
-            pl.BlockSpec(memory_space=pltpu.VMEM),
+        functools.partial(plan_body, dims=dims, col_size=col_size),
+        out_shape=(*lists, choice, choice, choice),
+        in_specs=[pl.BlockSpec(memory_space=pltpu.VMEM)],
+        out_specs=[pl.BlockSpec(memory_space=pltpu.VMEM)] * len(lists)
+        + [pl.BlockSpec(memory_space=pltpu.SMEM)] * 3,
+        scratch_shapes=[
+            *plan_scratch(dims, cols.shape[0]),
+            pltpu.VMEM((8, 128), I32),
+            pltpu.VMEM((col_size - 1, 8, 128), I32),
+            pltpu.SemaphoreType.DMA((col_size - 1,)),
+            pltpu.SemaphoreType.DMA((col_size - 1,)),
         ],
-        out_specs=[pl.BlockSpec(memory_space=pltpu.VMEM)] * 5,
-        scratch_shapes=[pltpu.VMEM((count, count), F32)],
+        compiler_params=pltpu.CompilerParams(collective_id=0, has_side_effects=True),
         name="plan",
-    )(rc, cols)
+    )(cols)
 
 
 def gather_body(index_ref, *refs, sizes):
@@ -344,12 +447,7 @@
     )(index, *sources)
 
 
-def ring_body(*refs, side, cols, stage, flags):
-    if flags:
-        send_ref, flag_ref, recv_ref, heard_ref = refs[:4]
-    else:
-        send_ref, recv_ref = refs[:2]
-    relay_up, relay_down, send_sem, recv_sem = refs[-4:]
+def ring_body(send_ref, recv_ref, relay_up, relay_down, send_sem, recv_sem, *, side, stage, cap):
     row, col = lax.axis_index("row"), lax.axis_index("col")
     hi, lo = row // side, lax.rem(row, side)
     low_axis = lax.rem(col + stage, 2)
@@ -360,14 +458,13 @@
         return (by_lo * (1 - low_axis) + by_hi * low_axis, col)
 
     right, left = along(1), along(side - 1)
-    peers = [(row, lax.rem(col + k, cols)) for k in range(1, cols)] if flags else []
     barrier = pltpu.get_barrier_semaphore()
-    for peer in [right, left, *peers]:
+    for peer in (right, left):
         pl.semaphore_signal(barrier, inc=1, device_id=peer, device_id_type=MESH)
-    pl.semaphore_wait(barrier, 2 + len(peers))
-
-    half = send_ref.shape[1] // 2
-    lower, upper = pl.ds(0, half), pl.ds(half, half)
+    pl.semaphore_wait(barrier, 2)
+
+    half = cap // 2
+    lower, upper, both = pl.ds(0, half), pl.ds(half, half), pl.ds(0, cap)
 
     def copy(n, src, dst, peer):
         return pltpu.make_async_remote_copy(
@@ -381,65 +478,79 @@
 
     far_up = copy(0, send_ref.at[1, lower], relay_up, right)
     far_down = copy(1, send_ref.at[1, upper], relay_down, left)
-    near_up = copy(2, send_ref.at[0], recv_ref.at[2], right)
-    near_down = copy(3, send_ref.at[2], recv_ref.at[0], left)
+    near_up = copy(2, send_ref.at[0, both], recv_ref.at[2, both], right)
+    near_down = copy(3, send_ref.at[2, both], recv_ref.at[0, both], left)
     next_up = copy(4, relay_up, recv_ref.at[1, lower], right)
     next_down = copy(5, relay_down, recv_ref.at[1, upper], left)
-    told = [copy(6 + k, flag_ref, heard_ref.at[k], peer) for k, peer in enumerate(peers)]
     far_up.start()
     far_down.start()
     near_up.start()
     near_down.start()
-    for one in told:
-        one.start()
     far_up.wait_recv()
     next_up.start()
     far_down.wait_recv()
     next_down.start()
     far_up.wait_send()
     far_down.wait_send()
-    for one in told:
-        one.wait()
     near_up.wait()
     near_down.wait()
     next_up.wait()
     next_down.wait()
 
 
-def ring(send, flag, side, cols, stage):
-    three, cap, *block = send.shape
-    flags = flag is not None
-    copies = 6 + (cols - 1 if flags else 0)
-    out_shape = [jax.ShapeDtypeStruct(send.shape, send.dtype)]
-    if flags:
-        out_shape.append(jax.ShapeDtypeStruct((cols - 1, *flag.shape), flag.dtype))
+def ring(send, side, stage, cap, collective_id):
+    block = send.shape[2:]
     return pl.pallas_call(
-        functools.partial(ring_body, side=side, cols=cols, stage=stage, flags=flags),
-        out_shape=out_shape,
-        in_specs=[pl.BlockSpec(memory_space=pl.ANY)] * (2 if flags else 1),
-        out_specs=[pl.BlockSpec(memory_space=pl.ANY)] * len(out_shape),
+        functools.partial(ring_body, side=side, stage=stage, cap=cap),
+        out_shape=jax.ShapeDtypeStruct(send.shape, send.dtype),
+        in_specs=[pl.BlockSpec(memory_space=pl.ANY)],
+        out_specs=pl.BlockSpec(memory_space=pl.ANY),
         scratch_shapes=[
             pltpu.VMEM((cap // 2, *block), send.dtype),
             pltpu.VMEM((cap // 2, *block), send.dtype),
-            pltpu.SemaphoreType.DMA((copies,)),
-            pltpu.SemaphoreType.DMA((copies,)),
+            pltpu.SemaphoreType.DMA((6,)),
+            pltpu.SemaphoreType.DMA((6,)),
         ],
-        compiler_params=pltpu.CompilerParams(collective_id=stage, has_side_effects=True),
+        compiler_params=pltpu.CompilerParams(collective_id=collective_id, has_side_effects=True),
         name="ring",
-    )(*([send, flag] if flags else [send]))
+    )(send)
+
+
+def ring_of(step, steps, send, side, stage, first_id):
+    choices = [
+        functools.partial(ring, side=side, stage=stage, cap=cap, collective_id=first_id + n)
+        for n, cap in enumerate(steps)
+    ]
+    return lax.switch(step, choices, send)
 
 
 def products_body(
     rc_ref, todo_ref, jobs_ref, band_ref, recv1_ref, recv2_ref, out_ref, held, half, acc, cube, jobs, sem, *, per
 ):
     n_band, n1, n2 = band_ref.shape[0], recv1_ref.shape[0], recv2_ref.shape[0]
-    copies = [
-        pltpu.make_async_copy(recv2_ref, held.at[pl.ds(n_band + 1 + n1, n2)], sem.at[2]),
-        pltpu.make_async_copy(recv1_ref, held.at[pl.ds(n_band + 1, n1)], sem.at[1]),
-        pltpu.make_async_copy(band_ref, held.at[pl.ds(0, n_band)], sem.at[0]),
-    ]
-    for one in copies:
-        one.start()
+    whole_band = pltpu.make_async_copy(band_ref, held.at[pl.ds(0, n_band)], sem.at[0])
+    lists, chunk = 3, 8
+
+    def received(action):
+        start = n_band + 1
+        for which, (ref, size) in enumerate(((recv1_ref, n1), (recv2_ref, n2))):
+            cap = size // lists
+            for d in range(lists):
+                here = todo_ref[0, 7, 1 + which * lists + d]
+                for at in range(d * cap, d * cap + cap, chunk):
+
+                    @pl.when(here > at - d * cap)
+                    def _(ref=ref, at=at, start=start):
+                        span = pl.ds(at, chunk)
+                        one = pltpu.make_async_copy(
+                            ref.at[span], held.at[pl.ds(start + at, chunk)], sem.at[1]
+                        )
+                        action(one)
+
+            start += size
+
+    whole_band.start()
+    received(lambda one: one.start())
     rows = out_ref.shape[0]
     tile = rows * per
     slots = n_band // rows
@@ -453,8 +564,8 @@
     def _():
         pltpu.sync_copy(jobs_ref, jobs)
 
-    for one in copies:
-        one.wait()
+    whole_band.wait()
+    received(lambda one: one.wait())
 
     def pair(left, which, m):
         a = [left[todo_ref[which, 2 + 2 * q, m]] for q in range(2)]
@@ -542,7 +653,7 @@
             pltpu.VMEM((band.shape[0] + 1, *block), F32),
             pltpu.VMEM((rows * per + 1, *block), F32),
             pltpu.SMEM(jobs.shape, I32),
-            pltpu.SemaphoreType.DMA((3,)),
+            pltpu.SemaphoreType.DMA((2,)),
         ],
         compiler_params=pltpu.CompilerParams(vmem_limit_bytes=60 * 1024 * 1024),
         name="products",
@@ -659,9 +770,9 @@
     row_size, col_size = sizes
     tile = lax.dynamic_slice_in_dim(density, rc[1] * per, per, 1)
     tile = tile.reshape(band_rows * per, *block)
-    panel = spread(tile, "row", row_size, 2).reshape(-1, *block)
+    panel = spread(tile, "row", row_size, 1).reshape(-1, *block)
     square = dense_step(rc, cols, density.reshape(-1, *block), panel, dims, False)
-    half = spread(square.astype(BF16), "col", col_size, 3).reshape(-1, *block)
+    half = spread(square.astype(BF16), "col", col_size, 2).reshape(-1, *block)
     cube = dense_step(rc, cols, half, panel, dims, True)
     return (3.0 * square - 2.0 * cube).astype(BF16).reshape(rows, per, *block)
 
@@ -675,21 +786,18 @@
     dims = (side, rows, width, per)
     rc = jnp.stack([lax.axis_index("row"), lax.axis_index("col")]).astype(I32)
     band = density.reshape(rows * slots, *block)
-    src1, src2, jobs, todo, flag = make_plan(rc, cols, dims)
+    src1, src2, jobs, todo, over, step1, step2 = make_plan(cols, dims, col_size)
     near = (side - 1) * CAP1
     far = (side - 1) * CAP2
-    packed = gather(src1, near, band)
-    recv1, heard = ring(packed.reshape(side - 1, CAP1, *block), flag, side, col_size, 0)
-    recv1 = recv1.reshape(near, *block)
-    packed = gather(src2, far, recv1, band)
-    (recv2,) = ring(packed.reshape(side - 1, CAP2, *block), None, side, col_size, 1)
-    recv2 = recv2.reshape(far, *block)
-    over = jnp.max(heard) + flag[0, 0] > 0
-    return lax.cond(
-        over,
-        lambda: dense(rc, cols, density, dims, sizes),
-        lambda: products(rc, todo, jobs, band, recv1, recv2, rows, per),
-    )
+
+    def sparse():
+        packed = gather(src1, near, band).reshape(side - 1, CAP1, *block)
+        recv1 = ring_of(step1[0], STEPS1, packed, side, 0, 3).reshape(near, *block)
+        packed = gather(src2, far, recv1, band).reshape(side - 1, CAP2, *block)
+        recv2 = ring_of(step2[0], STEPS2, packed, side, 1, 3 + len(STEPS1)).reshape(far, *block)
+        return products(rc, todo, jobs, band, recv1, recv2, rows, per)
+
+    return lax.cond(over[0] > 0, lambda: dense(rc, cols, density, dims, sizes), sparse)
 
 
 def solution(mesh):

time: 118 us -> 104 us (0.88); the launches traced: 117 us -> 106 us
  Pallas kernels: 112 us -> 102 us
  other arithmetic: 1.47 us -> 0.07 us
  loops' own time: 0.2 us -> 1.55 us
  local copies, waits for them, and re-layouts: 2.7 us -> 1.48 us
    pallas_call x3, Pallas kernels: 88 us -> 75.9 us  [the longest x2 58.3 us: ring(): pl.pallas_call(functools.partial(ring_body, side=side, stage=stage, cap=c...]
    pallas_call x1, Pallas kernels: 15 us -> 17.4 us  [products(): pl.pallas_call(functools.partial(products_body, per=per), out_shape=jax.S...]
    reduce_max x1 -> x0, other arithmetic: 1.39 us -> none  [local(): over = jnp.max(heard) + flag[0, 0] > 0]
    another operation x1 -> x3, loops' own time: 0.2 us -> 1.55 us  [the longest x1 1.48 us: local(): lax.cond(over[0] > 0, lambda: dense(rc, cols, density, dims, sizes), sparse)]
    slice x1 -> x0, local copies, waits for them, and re-layouts: 1.22 us -> none  [local(): over = jnp.max(heard) + flag[0, 0] > 0]
where the time goes in v4:
time: 104 us; the launch traced here: 106 us
  Pallas kernels  102 us (98%)
  loops' own time  1.55 us (1%)
  local copies, waits for them, and re-layouts  1.48 us (1%)
    pallas_call x2, Pallas kernels, ring(): pl.pallas_call(functools.partial(ring_body, side=side, stage=stage, cap=c...  58.3 us
    pallas_call x1, Pallas kernels, make_plan(): pl.pallas_call(functools.partial(plan_body, dims=dims, col_size=col_size)...  17.7 us
    pallas_call x1, Pallas kernels, products(): pl.pallas_call(functools.partial(products_body, per=per), out_shape=jax.S...  17.4 us
    pallas_call x2, Pallas kernels, gather(): pl.pallas_call(functools.partial(gather_body, sizes=tuple((s.shape[0] for...  8.62 us

profile of v4, /device:TPU:0, one launch (start us, length us, event | category | flops | bytes accessed | tf_op | source)
XLA Modules:
  0.0 105.8 jit_solution(6676229295491059023)
XLA Ops:
  0.0 0.1 pad_add_fusion
  0.1 1.5 %copy.5.cols_ref = s32[192,24]{1,0:T(8,128)} copy(s32[192,24]{0,1:T(8,128)} %param.13) | data formatting | bytes 36864 | tf_op args[1]
  1.6 17.7 %plan.1 = (s32[8,120]{1,0:T(8,128)S(1)}, s32[8,144]{1,0:T(8,128)S(1)}, s32[3,32,128]{2,1,0:T(8,128)S(1)}, s32[8,8,384]{2,1,0:T(8,128)S(1)}, s32[1]{0:T(128)}, /*index=5*/s32[1]{0:T(128)}, s32[1]{0:T(128)}) custom-call(s32[192,24]{1,0:T(8,128)} %copy.5.cols_ref), custom_call_target="tpu_custom_call" | custom-call | tf_op jit(solution)/shard_map/plan/pallas_call | solution.py:393
  19.8 85.8 %conditional.3 = (bf16[12,3,128,128]{3,2,1,0:T(8,128)(2,1)}) conditional(s32[]{:T(128)} %bitcast.26, (bf16[12,24,128,128]{3,2,1,0:T(8,128)(2,1)}, s32[1]{0:T(128)}, s32[8,120]{1,0:T(8,128)S(1)}, s32[1]{0:T(128)}, s32[8,144]{1,0:T(8,128)S(1)}, /*index=5*/s32[2]{0:T(128)S(1)}, s32[8,8,384]{2,1,0:T(8,128)S(1)}, s32[3,32,128]{2,1,0:T(8,128)S(1)}) %tuple.43, ...), branch_computations={%region_0.0_spmd, %region_9.0_spmd} | conditional | flops 17694724 | bytes 86151288 | solution.py:800
  21.1 3.9 %gather.2 = bf16[120,128,128]{2,1,0:T(8,128)(2,1)} custom-call(s32[8,120]{1,0:T(8,128)S(1)} %get-tuple-element.66.index_ref, bf16[288,128,128]{2,1,0:T(8,128)(2,1)} %bitcast.32), custom_call_target="tpu_custom_call" | custom-call | tf_op jit(solution)/shard_map/cond/branch_0_fun/gather/pallas_call | solution.py:439
  25.0 26.8 %conditional = (bf16[120,128,128]{2,1,0:T(8,128)(2,1)}) conditional(s32[]{:T(128)} %bitcast.17, bf16[120,128,128]{2,1,0:T(8,128)(2,1)} %gather.2, bf16[120,128,128]{2,1,0:T(8,128)(2,1)} %gather.2, bf16[120,128,128]{2,1,0:T(8,128)(2,1)} %gather.2, bf16[120,128,128]{2,1,0:T(8,128)(2,1)} %gather.2), branch_computations={%region_1.0_spmd, %region_2.0_spmd, %region_3.0_spmd, %region_4.0_... | conditional | bytes 8 | solution.py:524
  25.0 26.8 %ring.9 = bf16[3,40,128,128]{3,2,1,0:T(8,128)(2,1)} custom-call(bf16[3,40,128,128]{3,2,1,0:T(8,128)(2,1)} %bitcast.41), custom_call_target="tpu_custom_call" | custom-call | tf_op jit(solution)/shard_map/cond/branch_0_fun/cond/branch_1_fun/ring/pallas_call | solution.py:503
  51.8 4.7 %gather.3 = bf16[144,128,128]{2,1,0:T(8,128)(2,1)} custom-call(s32[8,144]{1,0:T(8,128)S(1)} %get-tuple-element.68.index_ref, bf16[120,128,128]{2,1,0:T(8,128)(2,1)} %get-tuple-element.94.refs_0_.recv1_ref, bf16[288,128,128]{2,1,0:T(8,128)(2,1)} %bitcast.33), custom_call_target="tpu_custom_call" | custom-call | tf_op jit(solution)/shard_map/cond/branch_0_fun/gather/pallas_call | solution.py:439
  56.5 31.5 %conditional.1 = (bf16[144,128,128]{2,1,0:T(8,128)(2,1)}) conditional(s32[]{:T(128)} %bitcast.18, bf16[144,128,128]{2,1,0:T(8,128)(2,1)} %gather.3, bf16[144,128,128]{2,1,0:T(8,128)(2,1)} %gather.3, bf16[144,128,128]{2,1,0:T(8,128)(2,1)} %gather.3, bf16[144,128,128]{2,1,0:T(8,128)(2,1)} %gather.3), branch_computations={%region_5.0_spmd, %region_6.0_spmd, %region_7.0_spmd, %region_8.0_... | conditional | bytes 8 | solution.py:524
  56.5 31.5 %ring.13 = bf16[3,48,128,128]{3,2,1,0:T(8,128)(2,1)} custom-call(bf16[3,48,128,128]{3,2,1,0:T(8,128)(2,1)} %bitcast.37), custom_call_target="tpu_custom_call" | custom-call | tf_op jit(solution)/shard_map/cond/branch_0_fun/cond/branch_1_fun/ring/pallas_call | solution.py:503
  88.1 17.4 %products.1 = bf16[12,3,128,128]{3,2,1,0:T(8,128)(2,1)} custom-call(s32[2]{0:T(128)S(1)} %get-tuple-element.61.rc_ref, s32[8,8,384]{2,1,0:T(8,128)S(1)} %get-tuple-element.62.todo_ref, s32[3,32,128]{2,1,0:T(8,128)S(1)} %get-tuple-element.63.jobs_ref, bf16[288,128,128]{2,1,0:T(8,128)(2,1)} %bitcast.34, ...), custom_call_target="tpu_custom_call" | custom-call | tf_op jit(solution)/shard_map/cond/branch_0_fun/products/pallas_call | solution.py:644
